TPU v7x, 512 devices: a whole 4x4x16 slice. The times are simulated.
512 devices in a mesh: chan: 64 (over z, x), tm: 8 (over y, core).
Axes of the slice: x: 4, y: 4, z: 16, core: 2. Of those that a mesh axis runs over, the one named last changes fastest.
Arguments:
- samples: bfloat16 [128, 2097152], P('chan', 'tm'), may hold values from -8 to 8
- taps: float32 [16, 4096], replicated, may hold values from -0.0234375 to 0.0234375
- steering: float32 [8, 128], replicated, may hold values from -6 to 6
- interferer_ids: int32 [2048, 4], P(('chan', 'tm')), may hold values from 0 to 7, all different within a row
- ranks: int32 [2048], P(('chan', 'tm')), may hold values from 0 to 4
Outputs:
- covariance: float32 [2048, 2, 128, 128], P(('chan', 'tm'))
Inputs may be any that keep to these rules, and one draw needn't show every extreme that they name: `interferer_ids`: the 4 entries of one channel's row name different directions.
All inputs are finite; a program needn't handle non-finite values.
Results may differ from a plain program's by a relative error of at most 0.00075.
Values may be sent and summed in bfloat16 or wider, within the bound.
A program may use at most 64 MiB of HBM per device.

v0:
```python
import jax
import jax.numpy as jnp
import numpy as np
from jax import lax
from jax.experimental import pallas as pl
from jax.experimental.pallas import tpu as pltpu
from jax.sharding import PartitionSpec as P

SLOW = 32
FAST = 128
EPSILON = 1e-06
F32 = jnp.float32
BF16 = jnp.bfloat16
HIGHEST = lax.Precision.HIGHEST


def split_constant(values):
    high = values.astype(np.float32).astype(jnp.bfloat16)
    low = (values - high.astype(np.float64)).astype(np.float32).astype(jnp.bfloat16)
    return high, low


def first_stage_matrix():
    p = np.arange(SLOW)
    rows = [np.ones(SLOW), (-1.0) ** p]
    for k1 in range(1, SLOW // 2):
        rows.append(np.cos(2.0 * np.pi * (k1 * p % SLOW) / SLOW))
        rows.append(-np.sin(2.0 * np.pi * (k1 * p % SLOW) / SLOW))
    coefficients = np.stack(rows)
    full = np.einsum("kp,fg->kfgp", coefficients, np.eye(8)).reshape(SLOW * 8, 8 * SLOW)
    return split_constant(full)


def second_stage_matrix():
    turns = np.outer(np.arange(64), np.arange(FAST)) % FAST
    angle = 2.0 * np.pi * turns / FAST
    real_rows = np.concatenate([np.cos(angle), np.sin(angle)], axis=1)
    imag_rows = np.concatenate([-np.sin(angle), np.cos(angle)], axis=1)
    high, low = split_constant(np.concatenate([real_rows, imag_rows], axis=0))
    return np.concatenate([high, low], axis=0)


def twiddles():
    angle = 2.0 * np.pi * np.outer(np.arange(SLOW), np.arange(FAST)) / (SLOW * FAST)
    return np.cos(angle).astype(np.float32), np.sin(angle).astype(np.float32)


def split(values):
    high = values.astype(BF16)
    return high, (values - high.astype(F32)).astype(BF16)


def dot(a, b):
    return lax.dot_general(a, b, (((1,), (0,)), ((), ())), preferred_element_type=F32)


def dot_t(a, b):
    return lax.dot_general(a, b, (((1,), (1,)), ((), ())), preferred_element_type=F32)


def channelize_kernel(now_ref, before_ref, taps_ref, w1h_ref, w1l_ref, w2_ref, cos_ref, sin_ref, out_ref,
                      window, filtered, y, spectrum):
    tap_count = taps_ref.shape[0]
    halo = tap_count - 1
    frames = now_ref.shape[0]
    rows = now_ref.shape[1]
    window[0:halo] = before_ref[...].astype(F32)

    def widen(g, carry):
        at = pl.multiple_of(g * 8, 8)
        window[pl.ds(halo + at, 8)] = now_ref[pl.ds(at, 8)].astype(F32)
        return carry

    lax.fori_loop(0, frames // 8, widen, 0)

    def group(g, carry):
        first = pl.multiple_of(g * 8, 8)
        for r in range(0, rows, 8):
            weights = [taps_ref[t, r : r + 8, :] for t in range(tap_count)]
            seen = [window[first + i, r : r + 8, :] for i in range(8 + halo)]
            for f in range(8):
                total = weights[0] * seen[f]
                for t in range(1, tap_count):
                    total = total + weights[t] * seen[f + t]
                filtered[f, r : r + 8, :] = total
        columns_h, columns_l = [], []
        for a in range(2):
            parts = [split(filtered[f, pl.ds(a, SLOW, stride=2), :]) for f in range(8)]
            columns_h.append(jnp.concatenate([h for h, _ in parts], axis=0))
            columns_l.append(jnp.concatenate([l for _, l in parts], axis=0))
        xh = jnp.concatenate(columns_h, axis=1)
        xl = jnp.concatenate(columns_l, axis=1)
        turned = dot(w1h_ref[...], xh) + dot(w1h_ref[...], xl) + dot(w1l_ref[...], xh)
        for a in range(2):
            piece = turned[:, a * FAST : (a + 1) * FAST].reshape(SLOW, 8, FAST)
            y[:, pl.ds(pl.multiple_of(a * frames + g * 8, 8), 8), :] = piece
        return carry

    lax.fori_loop(0, frames // 8, group, 0)

    w2 = w2_ref[...]
    w2h = w2[:FAST]

    def finish(zr, zi, k1):
        zh, zl = split(jnp.concatenate([zr, zi], axis=1))
        both = dot_t(w2, zh)
        result = both[:FAST] + both[FAST:] + dot_t(w2h, zl)
        for part in range(2):
            start = (k1 // 4) * 8 + part * 4 + k1 % 4
            spectrum[pl.ds(start, 64, stride=64), :] = result[part * 64 : (part + 1) * 64]

    for k1 in (0, SLOW // 2):
        real = y[0 if k1 == 0 else 1]
        finish(real * cos_ref[k1 : k1 + 1, :], -real * sin_ref[k1 : k1 + 1, :], k1)
    for k1 in range(1, SLOW // 2):
        real, imag = y[2 * k1], y[2 * k1 + 1]
        c, s = cos_ref[k1 : k1 + 1, :], sin_ref[k1 : k1 + 1, :]
        finish(real * c + imag * s, imag * c - real * s, k1)
        k1 = SLOW - k1
        c, s = cos_ref[k1 : k1 + 1, :], sin_ref[k1 : k1 + 1, :]
        finish(real * c - imag * s, -imag * c - real * s, k1)

    def pack(i, carry):
        at = pl.multiple_of(i * 32, 32)
        out_ref[pl.ds(at, 32)] = spectrum[pl.ds(pl.multiple_of(at * 8, 256), 256), :].reshape(32, 8, FAST).astype(BF16)
        return carry

    lax.fori_loop(0, 16, pack, 0)


def channelize(now, before, taps):
    frames, rows, _ = now.shape
    w1h, w1l = first_stage_matrix()
    cos, sin = twiddles()
    vmem = pl.BlockSpec(memory_space=pltpu.VMEM)
    return pl.pallas_call(
        channelize_kernel,
        out_shape=jax.ShapeDtypeStruct((512, 8, FAST), BF16),
        in_specs=[vmem] * 8,
        out_specs=vmem,
        scratch_shapes=[
            pltpu.VMEM((frames + before.shape[0], rows, FAST), F32),
            pltpu.VMEM((8, rows, FAST), F32),
            pltpu.VMEM((SLOW, 2 * frames, FAST), F32),
            pltpu.VMEM((4096, FAST), F32),
        ],
        compiler_params=pltpu.CompilerParams(vmem_limit_bytes=40 << 20),
        cost_estimate=pl.CostEstimate(flops=10**9, bytes_accessed=4 << 20, transcendentals=0),
    )(now, before, taps, jnp.asarray(w1h), jnp.asarray(w1l), jnp.asarray(second_stage_matrix()),
      jnp.asarray(cos), jnp.asarray(sin))


def exchange_kernel(extents, near, src_ref, dst_ref, send_sem, recv_sem, local_sem, plane_sem, whole_sem):
    nz, nx, ny, nc = extents
    nt = ny * nc
    total = nz * nx * nt
    group = lax.axis_index("chan")
    shard = lax.axis_index("tm")
    z, x = group // nx, lax.rem(group, nx)
    yy, core = shard // nc, lax.rem(shard, nc)
    me = shard * (nz * nx) + group

    def along_z(d):
        return {"chan": lax.rem(z + d, nz) * nx + x}

    def along_x(d):
        return {"chan": z * nx + lax.rem(x + d, nx)}

    def along_t(d):
        return {"tm": lax.rem(shard + d, nt)}

    barrier = pltpu.get_barrier_semaphore()
    for count, line in ((nz, along_z), (nx, along_x), (nt, along_t)):
        for d in range(1, count):
            pl.semaphore_signal(barrier, inc=1, device_id=line(d))
    pl.semaphore_wait(barrier, nz + nx + nt - 3)
    for d in range(1, nz):
        pl.semaphore_signal(plane_sem, inc=1, device_id=along_z(d))
    pl.semaphore_wait(plane_sem, nz - 1)
    for d in range(1, nx):
        pl.semaphore_signal(whole_sem, inc=1, device_id=along_x(d))
    pl.semaphore_wait(whole_sem, nx - 1)

    def send(dz, r):
        dx, dy, dc = lax.rem(r, nx), lax.rem(r // nx, ny), r // (nx * ny)
        to_group = lax.rem(z + dz, nz) * nx + lax.rem(x + dx, nx)
        to_shard = lax.rem(yy + dy, ny) * nc + lax.rem(core + dc, nc)
        pltpu.make_async_remote_copy(
            src_ref=src_ref.at[to_group * nt + to_shard],
            dst_ref=dst_ref.at[me],
            send_sem=send_sem,
            recv_sem=recv_sem,
            device_id={"chan": to_group, "tm": to_shard},
        ).start()

    for dz in near:
        if dz:
            send(dz, jnp.int32(0))

    def rest(r, carry):
        for dz in near:
            send(dz, r)
        return carry

    lax.fori_loop(1, nx * ny * nc, rest, 0)
    own = pltpu.make_async_copy(src_ref.at[group * nt + shard], dst_ref.at[me], local_sem)
    own.start()
    own.wait()
    others = pl.ds(0, total - 1)
    pltpu.make_async_copy(src_ref.at[others], src_ref.at[others], send_sem).wait()
    pltpu.make_async_copy(dst_ref.at[others], dst_ref.at[others], recv_sem).wait()


def exchange(pieces):
    extents = (16, 4, 4, 2)
    near = [8]
    for d in range(1, 8):
        near += [d, 16 - d]
    near.append(0)

    def kernel(*refs):
        exchange_kernel(extents, near, *refs)

    vmem = pl.BlockSpec(memory_space=pltpu.VMEM)
    return pl.pallas_call(
        kernel,
        out_shape=jax.ShapeDtypeStruct(pieces.shape, pieces.dtype),
        in_specs=[vmem],
        out_specs=vmem,
        scratch_shapes=[pltpu.SemaphoreType.DMA] * 3 + [pltpu.SemaphoreType.REGULAR] * 2,
        compiler_params=pltpu.CompilerParams(collective_id=0, has_side_effects=True, vmem_limit_bytes=16 << 20),
    )(pieces)


def orthonormal(vectors):
    found = []
    for column in range(vectors.shape[1]):
        residue = vectors[:, column, :]
        for earlier in found:
            residue = residue - earlier * jnp.sum(earlier * residue, axis=-1, keepdims=True)
        found.append(residue / jnp.sqrt(jnp.sum(residue * residue, axis=-1, keepdims=True) + EPSILON))
    return jnp.stack(found, axis=1)


def projectors(chosen, counted, steering):
    count, slots = chosen.shape
    directions, antennas = steering.shape
    onehot = (chosen[:, :, None] == lax.broadcasted_iota(jnp.int32, (count, slots, directions), 2)).astype(F32)
    live = (lax.broadcasted_iota(jnp.int32, (count, slots), 1) < counted[:, None]).astype(F32)
    vectors = jnp.einsum("crn,na->cra", onehot, steering, precision=HIGHEST) * live[:, :, None]
    basis = orthonormal(vectors)
    return jnp.eye(antennas, dtype=F32) - jnp.einsum("cra,crb->cab", basis, basis, precision=HIGHEST)


def covariance_kernel(frame_total, received_ref, projector_ref, out_ref, wide, rows):
    lane = lax.broadcasted_iota(jnp.int32, (64, FAST), 1)
    lower = lane < 64
    shards = received_ref.shape[0] // 64
    for t in range(shards):
        wide[pl.ds(t * 512, 512), :] = received_ref[pl.ds(t * 64, 64)].astype(F32).reshape(512, FAST)
    for channel in range(4):
        for part in range(2):
            for t in range(0, shards, 2):
                a = wide[pl.ds(t * 512 + part * 4 + channel, 64, stride=8), :]
                b = wide[pl.ds((t + 1) * 512 + part * 4 + channel, 64, stride=8), :]
                first = jnp.where(lower, a, pltpu.roll(b, 64, 1))
                second = jnp.where(lower, pltpu.roll(a, 64, 1), b)
                rows[t // 2, pl.ds(part * 128, 64, stride=2), :] = first
                rows[t // 2, pl.ds(part * 128 + 1, 64, stride=2), :] = second
        x = jnp.concatenate([rows[i].astype(BF16) for i in range(shards // 2)], axis=1)
        outer = dot_t(x, x)
        gram_real = outer[:128, :128] + outer[128:, 128:]
        gram_imag = outer[128:, :128] - outer[:128, 128:]
        keep = projector_ref[channel]
        left = jnp.dot(jnp.concatenate([gram_real, gram_imag], axis=0), keep, precision=HIGHEST, preferred_element_type=F32)
        both = jnp.concatenate([left[:128], left[128:]], axis=1)
        done = jnp.dot(keep, both, precision=HIGHEST, preferred_element_type=F32) * (1.0 / frame_total)
        out_ref[channel, 0] = done[:, :128]
        out_ref[channel, 1] = done[:, 128:]


def covariance(received, keep, frame_total):
    def kernel(*refs):
        covariance_kernel(frame_total, *refs)

    vmem = pl.BlockSpec(memory_space=pltpu.VMEM)
    return pl.pallas_call(
        kernel,
        out_shape=jax.ShapeDtypeStruct((4, 2, 128, 128), F32),
        in_specs=[vmem] * 2,
        out_specs=vmem,
        scratch_shapes=[pltpu.VMEM((4096, FAST), F32), pltpu.VMEM((4, 256, FAST), F32)],
        compiler_params=pltpu.CompilerParams(vmem_limit_bytes=24 << 20),
        cost_estimate=pl.CostEstimate(flops=10**9, bytes_accessed=2 << 20, transcendentals=0),
    )(received, keep)


def per_device(samples, taps, steering, interferer_ids, ranks):
    antennas, width = samples.shape
    tap_count, length = taps.shape
    frames = width // length
    peers = lax.axis_size("tm")
    blocks = samples.reshape(antennas, frames * SLOW, FAST).transpose(1, 0, 2).reshape(frames, SLOW * antennas, FAST)
    before = lax.ppermute(blocks[frames - tap_count + 1 :], "tm", [(i, i + 1) for i in range(peers - 1)])
    weights = jnp.repeat(taps.reshape(tap_count, SLOW, FAST), antennas, axis=1)
    pieces = channelize(blocks, before, weights)
    received = exchange(pieces)
    keep = projectors(interferer_ids, ranks, steering)
    return covariance(received, keep, frames * peers)


def solution(mesh):
    in_specs = (P("chan", "tm"), P(), P(), P(("chan", "tm"), None), P(("chan", "tm")))
    out_specs = P(("chan", "tm"), None, None, None)
    return jax.shard_map(per_device, mesh=mesh, in_specs=in_specs, out_specs=out_specs, check_vma=False)
```

profile of v0, /device:TPU:1, one launch (start us, length us, event | category | flops | bytes accessed | tf_op | source)
XLA Modules:
  0.0 96.5 jit_solution(8350209962035345668)
XLA Ops:
  0.0 0.0 copy-start
  0.0 0.0 copy-start.8
  0.0 0.0 copy-start.9
  0.0 0.0 copy-start.7
  0.0 1.2 %slice.24 = bf16[480,2,128]{2,1,0:T(2,128)(2,1)S(1)} slice(bf16[2048,2,128]{2,1,0:T(2,128)(2,1)} %bitcast.41), slice={[1568:2048], [0:2], [0:128]} | slice | bytes 491520 | tf_op jit(solution)/shard_map/slice | solution.py:304
  1.2 0.0 copy-start.1
  1.2 4.7 %collective-permute-start = (bf16[15,64,128]{2,1,0:T(8,128)(2,1)S(1)}, bf16[15,64,128]{2,1,0:T(8,128)(2,1)S(1)}, u32[]{:S(2)}, u32[]{:S(2)}) collective-permute-start(bf16[15,64,128]{2,1,0:T(8,128)(2,1)S(1)} %bitcast.45), channel_id=1, source_target_pairs={{0,1},{1,2},{2,3},{3,4},{4,5},{5,6},{6,7},{8,9},{9,10},{10,11},{11... | collective-permute-start | bytes 737288 | tf_op jit(solution)/shard_map/ppermute | solution.py:304
  5.9 0.0 copy-done.8
  6.0 0.1 iota_compare_fusion.1
  6.0 0.0 copy-done.9
  6.0 0.0 copy-done
  6.1 0.1 convolution_multiply_fusion
  6.2 0.1 fusion.7
  6.3 0.2 fusion.6
  6.5 0.2 fusion.4
  6.7 0.2 multiply_reduce_fusion.4
  6.9 0.2 multiply_reduce_fusion.2
  7.2 0.2 multiply_reduce_fusion.1
  7.3 0.2 multiply_reduce_fusion
  7.6 0.1 subtract_divide_fusion
  7.7 0.0 copy-done.7
  7.7 0.1 copy.22
  7.7 0.6 convolution_subtract_fusion.refs_1_
  8.3 2.1 %collective-permute-done.before_ref = bf16[15,64,128]{2,1,0:T(8,128)(2,1)S(1)} collective-permute-done((bf16[15,64,128]{2,1,0:T(8,128)(2,1)S(1)}, bf16[15,64,128]{2,1,0:T(8,128)(2,1)S(1)}, u32[]{:S(2)}, u32[]{:S(2)}) %collective-permute-start) | collective-permute-done | bytes 245792 | tf_op jit(solution)/shard_map/ppermute | solution.py:304
  10.5 0.0 copy-start.2
  10.5 0.0 copy-start.3
  10.5 0.0 copy-start.4
  10.5 0.0 copy-start.5
  10.5 0.0 copy-start.6
  10.5 0.2 broadcast_in_dim.2
  10.7 0.0 copy-done.1
  10.7 0.7 copy-done.2
  11.4 0.1 copy-done.3
  11.5 0.1 copy-done.4
  11.5 0.0 copy-done.5
  11.5 0.0 copy-done.6
  11.5 9.1 %shard_map.100.refs_0_ = bf16[512,8,128]{2,1,0:T(8,128)(2,1)S(1)} custom-call(bf16[64,64,128]{2,1,0:T(8,128)(2,1)S(1)} %bitcast.42, bf16[15,64,128]{2,1,0:T(8,128)(2,1)S(1)} %collective-permute-done.before_ref, f32[16,64,128]{2,1,0:T(8,128)S(1)} %bitcast.40, bf16[256,256]{1,0:T(8,128)(2,1)S(1)} %copy-done.2, bf16[256,256]{1,0:T(8,128)(2,1)S(1)} %copy-done.3, ...), custom_call_target="tpu_custom_call" | custom-call | flops 1000000000 | bytes 4194304 | tf_op jit(solution)/shard_map/pallas_call | solution.py:136
  20.7 72.2 %shard_map.101.refs_0_ = bf16[512,8,128]{2,1,0:T(8,128)(2,1)S(1)} custom-call(bf16[512,8,128]{2,1,0:T(8,128)(2,1)S(1)} %shard_map.100.refs_0_), custom_call_target="tpu_custom_call" | custom-call | tf_op jit(solution)/shard_map/pallas_call | solution.py:225
  92.9 3.6 %shard_map.102 = f32[4,2,128,128]{3,2,1,0:T(8,128)} custom-call(bf16[512,8,128]{2,1,0:T(8,128)(2,1)S(1)} %shard_map.101.refs_0_, f32[4,128,128]{2,1,0:T(8,128)S(1)} %convolution_subtract_fusion.refs_1_), custom_call_target="tpu_custom_call" | custom-call | flops 1000000000 | bytes 2097152 | tf_op jit(solution)/shard_map/pallas_call | solution.py:287
  (7 shorter events, 0.1 us)
Async XLA Ops:
  0.0 6.0 %copy-start = (f32[8,128]{1,0:T(8,128)S(1)}, f32[8,128]{1,0:T(8,128)}, u32[]{:S(2)}) copy-start(f32[8,128]{1,0:T(8,128)} %param.12) | copy-start | bytes 12292
  0.0 5.9 %copy-start.8 = (s32[4,4]{1,0:T(4,128)S(1)}, s32[4,4]{1,0:T(4,128)}, u32[]{:S(2)}) copy-start(s32[4,4]{1,0:T(4,128)} %param.13) | copy-start | bytes 196
  0.0 6.0 %copy-start.9 = (s32[4]{0:T(128)S(1)}, s32[4]{0:T(128)}, u32[]{:S(2)}) copy-start(s32[4]{0:T(128)} %param.14) | copy-start | bytes 52
  0.0 7.7 %copy-start.7 = (f32[16,4096]{1,0:T(8,128)S(1)}, f32[16,4096]{1,0:T(8,128)}, u32[]{:S(2)}) copy-start(f32[16,4096]{1,0:T(8,128)} %param.11) | copy-start | bytes 786436
  1.2 9.5 %copy-start.1 = (bf16[2,262144]{1,0:T(2,128)(2,1)S(1)}, bf16[2,262144]{1,0:T(2,128)(2,1)}, u32[]{:S(2)}) copy-start(bf16[2,262144]{1,0:T(2,128)(2,1)} %param.10) | copy-start | bytes 3145732
  1.2 9.3 %collective-permute-start = (bf16[15,64,128]{2,1,0:T(8,128)(2,1)S(1)}, bf16[15,64,128]{2,1,0:T(8,128)(2,1)S(1)}, u32[]{:S(2)}, u32[]{:S(2)}) collective-permute-start(bf16[15,64,128]{2,1,0:T(8,128)(2,1)S(1)} %bitcast.45), channel_id=1, source_target_pairs={{0,1},{1,2},{2,3},{3,4},{4,5},{5,6},{6,7},{8,9},{9,10},{10,11},{11... | collective-permute-start | bytes 737288 | tf_op jit(solution)/shard_map/ppermute | solution.py:304
  10.5 0.9 copy-start.2
  10.5 1.0 %copy-start.3 = (bf16[256,256]{1,0:T(8,128)(2,1)S(1)}, bf16[256,256]{1,0:T(8,128)(2,1)}, u32[]{:S(2)}) copy-start(bf16[256,256]{1,0:T(8,128)(2,1)} %constant.15.clone.w1l_ref) | copy-start | bytes 393220
  10.5 1.0 %copy-start.4 = (bf16[256,256]{1,0:T(8,128)(2,1)S(1)}, bf16[256,256]{1,0:T(8,128)(2,1)}, u32[]{:S(2)}) copy-start(bf16[256,256]{1,0:T(8,128)(2,1)} %constant.16.clone.w2_ref) | copy-start | bytes 393220
  10.5 1.0 %copy-start.5 = (f32[32,128]{1,0:T(8,128)S(1)}, f32[32,128]{1,0:T(8,128)}, u32[]{:S(2)}) copy-start(f32[32,128]{1,0:T(8,128)} %constant.17.clone.cos_ref) | copy-start | bytes 49156
  10.5 1.0 %copy-start.6 = (f32[32,128]{1,0:T(8,128)S(1)}, f32[32,128]{1,0:T(8,128)}, u32[]{:S(2)}) copy-start(f32[32,128]{1,0:T(8,128)} %constant.18.clone.sin_ref) | copy-start | bytes 49156
where the time goes:
time: 96.7 us; the launch traced here: 96.5 us
  Pallas kernels  84.9 us (88%)
  starting transfers between devices  4.73 us (5%)
  local copies, waits for them, and re-layouts  2.24 us (2%)
  waiting for transfers between devices  2.14 us (2%)
  other arithmetic  1.51 us (2%)
    pallas_call x1, Pallas kernels, exchange(): pl.pallas_call(kernel, out_shape=jax.ShapeDtypeStruct(pieces.shape, piece...  72.2 us
    pallas_call x1, Pallas kernels, channelize(): pl.pallas_call(channelize_kernel, out_shape=jax.ShapeDtypeStruct((512, 8,...  9.13 us
    ppermute x1, starting transfers between devices, per_device(): lax.ppermute(blocks[frames - tap_count + 1:], 'tm', [(i, i + 1) for i in...  4.73 us
    pallas_call x1, Pallas kernels, covariance(): pl.pallas_call(kernel, out_shape=jax.ShapeDtypeStruct((4, 2, 128, 128), F...  3.56 us
    ppermute x1, waiting for transfers between devices, per_device(): lax.ppermute(blocks[frames - tap_count + 1:], 'tm', [(i, i + 1) for i in...  2.14 us
  transfers between devices with their start and end apart: 1, of which 1 were waited for; matrix products, arithmetic and copies ran while one was open for 2% of the time, Pallas kernels for 0%

commit v1 on v0

v1 whole, which is shorter than its diff:
```python
import jax
import jax.numpy as jnp
import numpy as np
from jax import lax
from jax.experimental import pallas as pl
from jax.experimental.pallas import tpu as pltpu
from jax.sharding import PartitionSpec as P

SLOW = 32
FAST = 128
EPSILON = 1e-06
F32 = jnp.float32
BF16 = jnp.bfloat16
HIGHEST = lax.Precision.HIGHEST


def split_constant(values):
    high = values.astype(np.float32).astype(jnp.bfloat16)
    low = (values - high.astype(np.float64)).astype(np.float32).astype(jnp.bfloat16)
    return high, low


def first_stage_matrix():
    p = np.arange(SLOW)
    rows = []
    for k1 in range(SLOW // 2 + 1):
        angle = 2.0 * np.pi * (k1 * p % SLOW) / SLOW
        rows.append(np.cos(angle))
        rows.append(-np.sin(angle) if k1 % (SLOW // 2) else np.zeros(SLOW))
    coefficients = np.stack(rows)
    full = np.einsum("kp,fg->kfgp", coefficients, np.eye(8)).reshape(len(rows) * 8, 8 * SLOW)
    return split_constant(full)


def second_stage_matrix():
    turns = np.outer(np.arange(64), np.arange(FAST)) % FAST
    angle = 2.0 * np.pi * turns / FAST
    real_rows = np.concatenate([np.cos(angle), np.sin(angle)], axis=1)
    imag_rows = np.concatenate([-np.sin(angle), np.cos(angle)], axis=1)
    high, low = split_constant(np.concatenate([real_rows, imag_rows], axis=0))
    return np.concatenate([high, low], axis=0)


def twiddles():
    angle = 2.0 * np.pi * np.outer(np.arange(SLOW), np.arange(FAST)) / (SLOW * FAST)
    sign = np.where(np.arange(SLOW) > SLOW // 2, -1.0, 1.0)[:, None]
    return np.stack([np.cos(angle), np.sin(angle), sign * np.cos(angle), sign * np.sin(angle)]).astype(np.float32)


def split(values):
    high = values.astype(BF16)
    return high, (values - high.astype(F32)).astype(BF16)


def dot(a, b):
    return lax.dot_general(a, b, (((1,), (0,)), ((), ())), preferred_element_type=F32)


def dot_t(a, b):
    return lax.dot_general(a, b, (((1,), (1,)), ((), ())), preferred_element_type=F32)


def spectra_kernel(extents, near, now_ref, taps_ref, w1_ref, w2_ref, table_ref, steering_ref, chosen_ref, counted_ref,
                   dst_ref, basis_ref, arrived, window, weights, filtered, y, spectrum, pieces, w1, w2, table,
                   in_sem, const_sem, halo_send, halo_recv, send_sem, recv_sem, local_sem, plane_sem, whole_sem):
    nz, nx, ny, nc = extents
    nt = ny * nc
    total = nz * nx * nt
    tap_count = taps_ref.shape[0]
    halo = tap_count - 1
    frames, rows, _ = now_ref.shape
    group = lax.axis_index("chan")
    shard = lax.axis_index("tm")
    z, x = group // nx, lax.rem(group, nx)
    me = shard * (nz * nx) + group

    def along_z(d):
        return {"chan": lax.rem(z + d, nz) * nx + x}

    def along_x(d):
        return {"chan": z * nx + lax.rem(x + d, nx)}

    def along_t(d):
        return {"tm": lax.rem(shard + d, nt)}

    constants = [
        pltpu.make_async_copy(source, target, const_sem.at[i])
        for i, (source, target) in enumerate(((w1_ref, w1), (w2_ref, w2), (table_ref, table)))
    ]
    inputs = [
        pltpu.make_async_copy(now_ref.at[pl.ds(i * 16, 16)], arrived.at[pl.ds(halo + i * 16, 16)], in_sem.at[i])
        for i in range(frames // 16)
    ]
    for copy in inputs + constants:
        copy.start()

    barrier = pltpu.get_barrier_semaphore()
    for count, line in ((nt, along_t), (nz, along_z), (nx, along_x)):
        for d in range(1, count):
            pl.semaphore_signal(barrier, inc=1, device_id=line(d))

    for a in range(2):
        for t in range(tap_count):
            weights[t, pl.ds(a, SLOW, stride=2), :] = taps_ref[t]

    @pl.when(shard == 0)
    def _():
        arrived[0:halo] = jnp.zeros((halo, rows, FAST), BF16)

    pl.semaphore_wait(barrier, nz + nx + nt - 3)
    carried = pltpu.make_async_remote_copy(
        src_ref=now_ref.at[pl.ds(frames - halo, halo)],
        dst_ref=arrived.at[pl.ds(0, halo)],
        send_sem=halo_send,
        recv_sem=halo_recv,
        device_id=along_t(1),
    )

    @pl.when(shard < nt - 1)
    def _():
        carried.start()

    for d in range(1, nz):
        pl.semaphore_signal(plane_sem, inc=1, device_id=along_z(d))

    for i, copy in enumerate(inputs):
        copy.wait()

        def widen(g, carry, i=i):
            at = halo + i * 16 + g * 8
            window[pl.ds(at, 8)] = arrived[pl.ds(at, 8)].astype(F32)
            return carry

        lax.fori_loop(0, 2, widen, 0)

    def filter_group(g, carry):
        first = pl.multiple_of(g * 8, 8)
        for r in range(0, rows, 8):
            tap = [weights[t, r : r + 8, :] for t in range(tap_count)]
            seen = [window[first + i, r : r + 8, :] for i in range(8 + halo)]
            for f in range(8):
                result = tap[0] * seen[f]
                for t in range(1, tap_count):
                    result = result + tap[t] * seen[f + t]
                filtered[f, r : r + 8, :] = result
        columns_h, columns_l = [], []
        for a in range(2):
            parts = [split(filtered[f, pl.ds(a, SLOW, stride=2), :]) for f in range(8)]
            columns_h.append(jnp.concatenate([h for h, _ in parts], axis=0))
            columns_l.append(jnp.concatenate([l for _, l in parts], axis=0))
        xh = jnp.concatenate(columns_h, axis=1)
        xl = jnp.concatenate(columns_l, axis=1)
        turned = dot(w1[0], xh) + dot(w1[0], xl) + dot(w1[1], xh)
        for a in range(2):
            piece = turned[:, a * FAST : (a + 1) * FAST].reshape(SLOW + 2, 8, FAST)
            y[:, pl.ds(pl.multiple_of(a * frames + g * 8, 8), 8), :] = piece
        return carry

    constants[0].wait()
    lax.fori_loop(2, 5, filter_group, 0)
    pl.semaphore_wait(plane_sem, nz - 1)
    for d in range(1, nx):
        pl.semaphore_signal(whole_sem, inc=1, device_id=along_x(d))
    lax.fori_loop(5, 8, filter_group, 0)

    @pl.when(shard > 0)
    def _():
        carried.wait_recv()

    @pl.when(shard < nt - 1)
    def _():
        carried.wait_send()

    window[0:halo] = arrived[0:halo].astype(F32)
    lax.fori_loop(0, 2, filter_group, 0)
    pl.semaphore_wait(whole_sem, nx - 1)
    constants[1].wait()
    constants[2].wait()
    own = pltpu.make_async_copy(pieces.at[group], dst_ref.at[me], local_sem)

    def finish(i, carry):
        to_shard = lax.rem(shard + i, nt)
        for sub in range(4):
            k1 = to_shard * 4 + sub
            j = jnp.minimum(k1, SLOW - k1)
            real, imag = y[2 * j], y[2 * j + 1]
            cos, sin, signed_cos, signed_sin = (table[n, pl.ds(k1, 1), :] for n in range(4))
            zr = real * cos + imag * signed_sin
            zi = imag * signed_cos - real * sin
            zh, zl = split(jnp.concatenate([zr, zi], axis=1))
            both = dot_t(w2[...], zh)
            result = both[:FAST] + both[FAST:] + dot_t(w2[:FAST], zl)
            for part in range(2):
                spectrum[pl.ds(part * 4 + sub, 64, stride=8), :] = result[part * 64 : (part + 1) * 64]
        base = pl.multiple_of(i * 64, 64)
        pieces[pl.ds(base, 64)] = spectrum[...].reshape(64, 8, FAST).astype(BF16)

        def send(dz, dx):
            to_group = lax.rem(z + dz, nz) * nx + lax.rem(x + dx, nx)
            pltpu.make_async_remote_copy(
                src_ref=pieces.at[base + to_group],
                dst_ref=dst_ref.at[me],
                send_sem=send_sem,
                recv_sem=recv_sem,
                device_id={"chan": to_group, "tm": to_shard},
            ).start()

        def column(dx, inner):
            for dz in near:
                if dz:
                    send(dz, dx)
                else:

                    @pl.when(i + dx > 0)
                    def _():
                        send(0, dx)

            return inner

        lax.fori_loop(0, nx, column, 0)
        return carry

    lax.fori_loop(0, nt, finish, 0)
    own.start()

    found = []
    for slot in range(chosen_ref.shape[1]):
        wanted = chosen_ref[:, slot : slot + 1]
        residue = jnp.zeros((chosen_ref.shape[0], FAST), F32)
        for direction in range(steering_ref.shape[0]):
            residue = jnp.where(wanted == direction, steering_ref[direction : direction + 1, :], residue)
        residue = jnp.where(counted_ref[...] > slot, residue, 0.0)
        for earlier in found:
            residue = residue - earlier * jnp.sum(earlier * residue, axis=-1, keepdims=True)
        found.append(residue / jnp.sqrt(jnp.sum(residue * residue, axis=-1, keepdims=True) + EPSILON))
    for slot, vector in enumerate(found):
        for channel in range(chosen_ref.shape[0]):
            basis_ref[channel, slot : slot + 1, :] = vector[channel : channel + 1, :]

    own.wait()
    others = pl.ds(0, total - 1)
    pltpu.make_async_copy(pieces.at[others], pieces.at[others], send_sem).wait()
    pltpu.make_async_copy(dst_ref.at[others], dst_ref.at[others], recv_sem).wait()


def spectra(now, taps, steering, chosen, counted):
    extents = (16, 4, 4, 2)
    near = [8]
    for d in range(1, 8):
        near += [d, 16 - d]
    near.append(0)

    def kernel(*refs):
        spectra_kernel(extents, near, *refs)

    frames, rows, _ = now.shape
    tap_count = taps.shape[0]
    w1 = np.stack(first_stage_matrix())
    w2 = second_stage_matrix()
    table = twiddles()
    vmem = pl.BlockSpec(memory_space=pltpu.VMEM)
    anywhere = pl.BlockSpec(memory_space=pl.ANY)
    dma = pltpu.SemaphoreType.DMA
    return pl.pallas_call(
        kernel,
        out_shape=(
            jax.ShapeDtypeStruct((512, 8, FAST), BF16),
            jax.ShapeDtypeStruct((chosen.shape[0], chosen.shape[1], FAST), F32),
        ),
        in_specs=[anywhere, vmem, anywhere, anywhere, anywhere, vmem, vmem, vmem],
        out_specs=(vmem, vmem),
        scratch_shapes=[
            pltpu.VMEM((frames + tap_count - 1, rows, FAST), BF16),
            pltpu.VMEM((frames + tap_count - 1, rows, FAST), F32),
            pltpu.VMEM((tap_count, rows, FAST), F32),
            pltpu.VMEM((8, rows, FAST), F32),
            pltpu.VMEM((SLOW + 2, 2 * frames, FAST), F32),
            pltpu.VMEM((512, FAST), F32),
            pltpu.VMEM((512, 8, FAST), BF16),
            pltpu.VMEM(w1.shape, BF16),
            pltpu.VMEM(w2.shape, BF16),
            pltpu.VMEM(table.shape, F32),
            dma((frames // 16,)),
            dma((3,)),
            dma,
            dma,
            dma,
            dma,
            dma,
            pltpu.SemaphoreType.REGULAR,
            pltpu.SemaphoreType.REGULAR,
        ],
        compiler_params=pltpu.CompilerParams(collective_id=0, has_side_effects=True, vmem_limit_bytes=40 << 20),
        cost_estimate=pl.CostEstimate(flops=10**9, bytes_accessed=4 << 20, transcendentals=0),
    )(now, taps, jnp.asarray(w1), jnp.asarray(w2), jnp.asarray(table), steering, chosen, counted)


def covariance_kernel(frame_total, received_ref, basis_ref, out_ref, wide, rows):
    lane = lax.broadcasted_iota(jnp.int32, (64, FAST), 1)
    lower = lane < 64
    identity = (
        lax.broadcasted_iota(jnp.int32, (128, 128), 0) == lax.broadcasted_iota(jnp.int32, (128, 128), 1)
    ).astype(F32)
    shards = received_ref.shape[0] // 64
    for t in range(shards):
        wide[pl.ds(t * 512, 512), :] = received_ref[pl.ds(t * 64, 64)].astype(F32).reshape(512, FAST)
    for channel in range(4):
        for part in range(2):
            for t in range(0, shards, 2):
                a = wide[pl.ds(t * 512 + part * 4 + channel, 64, stride=8), :]
                b = wide[pl.ds((t + 1) * 512 + part * 4 + channel, 64, stride=8), :]
                first = jnp.where(lower, a, pltpu.roll(b, 64, 1))
                second = jnp.where(lower, pltpu.roll(a, 64, 1), b)
                rows[t // 2, pl.ds(part * 128, 64, stride=2), :] = first
                rows[t // 2, pl.ds(part * 128 + 1, 64, stride=2), :] = second
        x = jnp.concatenate([rows[i].astype(BF16) for i in range(shards // 2)], axis=1)
        outer = dot_t(x, x)
        gram_real = outer[:128, :128] + outer[128:, 128:]
        gram_imag = outer[128:, :128] - outer[:128, 128:]
        basis = basis_ref[channel]
        keep = identity - lax.dot_general(
            basis, basis, (((0,), (0,)), ((), ())), precision=HIGHEST, preferred_element_type=F32
        )
        left = jnp.dot(jnp.concatenate([gram_real, gram_imag], axis=0), keep, precision=HIGHEST, preferred_element_type=F32)
        both = jnp.concatenate([left[:128], left[128:]], axis=1)
        done = jnp.dot(keep, both, precision=HIGHEST, preferred_element_type=F32) * (1.0 / frame_total)
        out_ref[channel, 0] = done[:, :128]
        out_ref[channel, 1] = done[:, 128:]


def covariance(received, basis, frame_total):
    def kernel(*refs):
        covariance_kernel(frame_total, *refs)

    vmem = pl.BlockSpec(memory_space=pltpu.VMEM)
    return pl.pallas_call(
        kernel,
        out_shape=jax.ShapeDtypeStruct((4, 2, 128, 128), F32),
        in_specs=[vmem] * 2,
        out_specs=vmem,
        scratch_shapes=[pltpu.VMEM((4096, FAST), F32), pltpu.VMEM((4, 256, FAST), F32)],
        compiler_params=pltpu.CompilerParams(vmem_limit_bytes=24 << 20),
        cost_estimate=pl.CostEstimate(flops=10**9, bytes_accessed=2 << 20, transcendentals=0),
    )(received, basis)


def per_device(samples, taps, steering, interferer_ids, ranks):
    antennas, width = samples.shape
    tap_count, length = taps.shape
    frames = width // length
    peers = lax.axis_size("tm")
    blocks = samples.reshape(antennas, frames * SLOW, FAST).transpose(1, 0, 2).reshape(frames, SLOW * antennas, FAST)
    received, basis = spectra(
        blocks, taps.reshape(tap_count, SLOW, FAST), steering, interferer_ids, ranks.reshape(-1, 1)
    )
    return covariance(received, basis, frames * peers)


def solution(mesh):
    in_specs = (P("chan", "tm"), P(), P(), P(("chan", "tm"), None), P(("chan", "tm")))
    out_specs = P(("chan", "tm"), None, None, None)
    return jax.shard_map(per_device, mesh=mesh, in_specs=in_specs, out_specs=out_specs, check_vma=False)
```

time: 96.7 us -> 85.2 us (0.88)
  starting transfers between devices: 4.73 us -> 0 us
  Pallas kernels: 84.9 us -> 81.9 us
  waiting for transfers between devices: 2.14 us -> 0 us
  other arithmetic: 1.51 us -> 0 us
    ppermute x1 -> x0, starting transfers between devices: 4.73 us -> none  [per_device(): lax.ppermute(blocks[frames - tap_count + 1:], 'tm', [(i, i + 1) for i in...]
    pallas_call x2 -> x1, Pallas kernels: 81.4 us -> 77.6 us  [spectra(): pl.pallas_call(kernel, out_shape=(jax.ShapeDtypeStruct((512, 8, FAST), BF...]
    ppermute x1 -> x0, waiting for transfers between devices: 2.14 us -> none  [per_device(): lax.ppermute(blocks[frames - tap_count + 1:], 'tm', [(i, i + 1) for i in...]
    unnamed x21 -> x13, local copies, waits for them, and re-layouts: 0.9 us -> 2.29 us
    reduce_sum x7 -> x0, other arithmetic: 1.29 us -> none  [the longest x5 0.98 us: orthonormal(): jnp.sum(earlier * residue, axis=-1, keepdims=True)]
    slice x1 -> x0, local copies, waits for them, and re-layouts: 1.16 us -> none  [per_device(): blocks[frames - tap_count + 1:]]
  transfers between devices with their start and end apart: 1 -> 0, of which waited for: 1 -> 0; matrix products, arithmetic and copies ran while one was open for 2% -> 0% of each run, Pallas kernels for 0% -> 0%
where the time goes in v1:
time: 85.2 us; the launch traced here: 85 us
  Pallas kernels  81.9 us (96%)
  local copies, waits for them, and re-layouts  3.07 us (4%)
    pallas_call x1, Pallas kernels, spectra(): pl.pallas_call(kernel, out_shape=(jax.ShapeDtypeStruct((512, 8, FAST), BF...  77.6 us
    pallas_call x1, Pallas kernels, covariance(): pl.pallas_call(kernel, out_shape=jax.ShapeDtypeStruct((4, 2, 128, 128), F...  4.25 us
    unnamed x13, local copies, waits for them, and re-layouts  2.29 us

profile of v1, /device:TPU:1, one launch (start us, length us, event | category | flops | bytes accessed | tf_op | source)
XLA Modules:
  0.0 85.0 jit_solution(13088060008431523879)
XLA Ops:
  0.0 0.0 copy-start.3
  0.0 0.8 copy.10.refs_7_
  0.8 0.0 copy-start.1
  0.8 0.0 copy-start.2
  0.8 0.0 copy-start.4
  0.8 0.0 copy-start.5
  0.8 1.0 %copy.11 = f32[2,8,32,128]{3,2,1,0:T(8,128)S(1)} copy(f32[2,8,32,128]{3,1,2,0:T(8,128)} %bitcast.10) | data formatting | bytes 524288
  1.8 0.0 copy-done.3
  1.9 0.0 copy-done.1
  1.9 0.0 copy-done.2
  1.9 0.0 copy-done.4
  1.9 0.0 copy-done.5
  1.9 0.0 copy-start
  1.9 1.2 %copy-done = bf16[2,262144]{1,0:T(2,128)(2,1)S(1)} copy-done((bf16[2,262144]{1,0:T(2,128)(2,1)S(1)}, bf16[2,262144]{1,0:T(2,128)(2,1)}, u32[]{:S(2)}) %copy-start) | copy-done | bytes 1048600
  3.1 77.6 %shard_map.82 = (bf16[512,8,128]{2,1,0:T(8,128)(2,1)S(1)}, f32[4,4,128]{2,1,0:T(4,128)S(1)}) custom-call(bf16[64,64,128]{2,1,0:T(8,128)(2,1)S(1)} %bitcast.9, f32[16,32,128]{2,1,0:T(8,128)S(1)} %bitcast.8, bf16[2,272,256]{2,1,0:T(8,128)(2,1)S(1)} %copy-done.3, bf16[256,256]{1,0:T(8,128)(2,1)S(1)} %copy-done.4, f32[4,32,128]{2,1,0:T(8,128)S(1)} %copy-done.5, ...), custom_call_target="tpu_custom_call" | custom-call | flops 1000000000 | bytes 4194304 | tf_op jit(solution)/shard_map/pallas_call | solution.py:264
  80.8 4.3 %shard_map.83 = f32[4,2,128,128]{3,2,1,0:T(8,128)} custom-call(bf16[512,8,128]{2,1,0:T(8,128)(2,1)S(1)} %get-tuple-element.7.refs_0_, f32[4,4,128]{2,1,0:T(4,128)S(1)} %get-tuple-element.8.refs_1_), custom_call_target="tpu_custom_call" | custom-call | flops 1000000000 | bytes 2097152 | tf_op jit(solution)/shard_map/pallas_call | solution.py:336
Async XLA Ops:
  0.0 1.9 %copy-start.3 = (bf16[2,272,256]{2,1,0:T(8,128)(2,1)S(1)}, bf16[2,272,256]{2,1,0:T(8,128)(2,1)}, u32[]{:S(2)}) copy-start(bf16[2,272,256]{2,1,0:T(8,128)(2,1)} %constant.6.clone.refs_2_) | copy-start | bytes 835588
  0.8 1.1 %copy-start.1 = (f32[8,128]{1,0:T(8,128)S(1)}, f32[8,128]{1,0:T(8,128)}, u32[]{:S(2)}) copy-start(f32[8,128]{1,0:T(8,128)} %refs_5_.1) | copy-start | bytes 12292
  0.8 1.1 %copy-start.2 = (s32[4,4]{1,0:T(4,128)S(1)}, s32[4,4]{1,0:T(4,128)}, u32[]{:S(2)}) copy-start(s32[4,4]{1,0:T(4,128)} %refs_6_.1) | copy-start | bytes 196
  0.8 1.1 %copy-start.4 = (bf16[256,256]{1,0:T(8,128)(2,1)S(1)}, bf16[256,256]{1,0:T(8,128)(2,1)}, u32[]{:S(2)}) copy-start(bf16[256,256]{1,0:T(8,128)(2,1)} %constant.7.clone.refs_3_) | copy-start | bytes 393220
  0.8 1.1 %copy-start.5 = (f32[4,32,128]{2,1,0:T(8,128)S(1)}, f32[4,32,128]{2,1,0:T(8,128)}, u32[]{:S(2)}) copy-start(f32[4,32,128]{2,1,0:T(8,128)} %constant.8.clone.refs_4_) | copy-start | bytes 196612
  1.9 1.2 %copy-start = (bf16[2,262144]{1,0:T(2,128)(2,1)S(1)}, bf16[2,262144]{1,0:T(2,128)(2,1)}, u32[]{:S(2)}) copy-start(bf16[2,262144]{1,0:T(2,128)(2,1)} %param.8) | copy-start | bytes 3145732

commit v2 on v1

v2 whole, which is shorter than its diff:
```python
import jax
import jax.numpy as jnp
import numpy as np
from jax import lax
from jax.experimental import pallas as pl
from jax.experimental.pallas import tpu as pltpu
from jax.sharding import PartitionSpec as P

SLOW = 32
FAST = 128
EPSILON = 1e-06
F32 = jnp.float32
BF16 = jnp.bfloat16
HIGHEST = lax.Precision.HIGHEST


def split_constant(values):
    high = values.astype(np.float32).astype(jnp.bfloat16)
    low = (values - high.astype(np.float64)).astype(np.float32).astype(jnp.bfloat16)
    return high, low


def first_stage_matrix():
    p = np.arange(SLOW)
    rows = []
    for k1 in range(SLOW // 2 + 1):
        angle = 2.0 * np.pi * (k1 * p % SLOW) / SLOW
        rows.append(np.cos(angle))
        rows.append(-np.sin(angle) if k1 % (SLOW // 2) else np.zeros(SLOW))
    coefficients = np.stack(rows)
    full = np.einsum("kp,fg->kfgp", coefficients, np.eye(8)).reshape(len(rows) * 8, 8 * SLOW)
    return split_constant(full)


def second_stage_matrix():
    turns = np.outer(np.arange(64), np.arange(FAST)) % FAST
    angle = 2.0 * np.pi * turns / FAST
    real_rows = np.concatenate([np.cos(angle), np.sin(angle)], axis=1)
    imag_rows = np.concatenate([-np.sin(angle), np.cos(angle)], axis=1)
    high, low = split_constant(np.concatenate([real_rows, imag_rows], axis=0))
    return np.concatenate([high, low], axis=0)


def twiddles():
    angle = 2.0 * np.pi * np.outer(np.arange(SLOW), np.arange(FAST)) / (SLOW * FAST)
    sign = np.where(np.arange(SLOW) > SLOW // 2, -1.0, 1.0)[:, None]
    return np.stack([np.cos(angle), np.sin(angle), sign * np.cos(angle), sign * np.sin(angle)]).astype(np.float32)


def split(values):
    high = values.astype(BF16)
    return high, (values - high.astype(F32)).astype(BF16)


def dot(a, b):
    return lax.dot_general(a, b, (((1,), (0,)), ((), ())), preferred_element_type=F32)


def dot_t(a, b):
    return lax.dot_general(a, b, (((1,), (1,)), ((), ())), preferred_element_type=F32)


def covariance_kernel(extents, near, now_ref, taps_ref, w1_ref, w2_ref, table_ref, steering_ref, chosen_ref, counted_ref,
                      out_ref, arrived, window, taps, weights, filtered, y, spectrum, pieces, landed, wide, sides,
                      gram_ref, keep_ref, done, w1, w2, table, in_sem, const_sem, halo_send, halo_recv, send_sem, recv_sem,
                      line_sem, whole_sem, out_sem):
    nz, nx, ny, nc = extents
    nt = ny * nc
    groups = nz * nx
    tap_count = taps_ref.shape[0]
    halo = tap_count - 1
    frames, rows, _ = now_ref.shape
    channels, slots = chosen_ref.shape
    group = lax.axis_index("chan")
    shard = lax.axis_index("tm")
    z, x = group // nx, lax.rem(group, nx)

    def along_z(d):
        return {"chan": lax.rem(z + d, nz) * nx + x}

    def along_x(d):
        return {"chan": z * nx + lax.rem(x + d, nx)}

    def along_t(d):
        return {"tm": lax.rem(shard + d, nt)}

    constants = [
        pltpu.make_async_copy(source, target, const_sem.at[i])
        for i, (source, target) in enumerate(((taps_ref, taps), (w1_ref, w1), (w2_ref, w2), (table_ref, table)))
    ]
    inputs = [
        pltpu.make_async_copy(now_ref.at[pl.ds(i * 16, 16)], arrived.at[pl.ds(halo + i * 16, 16)], in_sem.at[i])
        for i in range(frames // 16)
    ]
    for copy in constants[:1] + inputs + constants[1:]:
        copy.start()

    barrier = pltpu.get_barrier_semaphore()
    for count, line in ((nz, along_z), (nt, along_t), (nx, along_x)):
        for d in range(1, count):
            pl.semaphore_signal(barrier, inc=1, device_id=line(d))

    @pl.when(shard == 0)
    def _():
        arrived[0:halo] = jnp.zeros((halo, rows, FAST), BF16)

    constants[0].wait()
    for p in range(SLOW):
        for t in range(0, tap_count, 8):
            tile = taps[t : t + 8, p * FAST : (p + 1) * FAST]
            for a in range(2):
                weights[pl.ds(t * rows + 2 * p + a, 8, stride=rows), :] = tile

    def widen(i):
        inputs[i].wait()

        def convert(g, carry):
            at = halo + i * 16 + g * 8
            window[pl.ds(at, 8)] = arrived[pl.ds(at, 8)].astype(F32)
            return carry

        lax.fori_loop(0, 2, convert, 0)

    def filter_group(g):
        for r in range(0, rows, 8):
            tap = [weights[t * rows + r : t * rows + r + 8, :] for t in range(tap_count)]
            seen = [window[g * 8 + i, r : r + 8, :] for i in range(8 + halo)]
            for f in range(8):
                result = tap[0] * seen[f]
                for t in range(1, tap_count):
                    result = result + tap[t] * seen[f + t]
                filtered[g % 2, f, r : r + 8, :] = result

    def turn_group(g):
        columns_h, columns_l = [], []
        for a in range(2):
            parts = [split(filtered[g % 2, f, pl.ds(a, SLOW, stride=2), :]) for f in range(8)]
            columns_h.append(jnp.concatenate([h for h, _ in parts], axis=0))
            columns_l.append(jnp.concatenate([l for _, l in parts], axis=0))
        xh = jnp.concatenate(columns_h, axis=1)
        xl = jnp.concatenate(columns_l, axis=1)
        size = (SLOW + 2) * 8
        both = dot(w1[...], xh)
        turned = both[:size] + both[size:] + dot(w1[:size], xl)
        for a in range(2):
            piece = turned[:, a * FAST : (a + 1) * FAST].reshape(SLOW + 2, 8, FAST)
            y[:, a * frames + g * 8 : a * frames + g * 8 + 8, :] = piece

    widen(0)
    widen(1)
    filter_group(2)
    constants[1].wait()
    widen(2)
    filter_group(3)
    turn_group(2)
    widen(3)

    pl.semaphore_wait(barrier, nz + nx + nt - 3)
    carried = pltpu.make_async_remote_copy(
        src_ref=now_ref.at[pl.ds(frames - halo, halo)],
        dst_ref=arrived.at[pl.ds(0, halo)],
        send_sem=halo_send,
        recv_sem=halo_recv,
        device_id=along_t(1),
    )

    @pl.when(shard < nt - 1)
    def _():
        carried.start()

    for d in range(1, nt):
        pl.semaphore_signal(line_sem, inc=1, device_id=along_t(d))

    filter_group(4)
    turn_group(3)
    filter_group(5)
    turn_group(4)
    pl.semaphore_wait(line_sem, nt - 1)
    for d in range(1, nx):
        pl.semaphore_signal(whole_sem, inc=1, device_id=along_x(d))
    filter_group(6)
    turn_group(5)
    filter_group(7)
    turn_group(6)

    @pl.when(shard > 0)
    def _():
        carried.wait_recv()

    @pl.when(shard < nt - 1)
    def _():
        carried.wait_send()

    window[0:halo] = arrived[0:halo].astype(F32)
    filter_group(0)
    turn_group(7)
    filter_group(1)
    turn_group(0)
    turn_group(1)
    pl.semaphore_wait(whole_sem, nx - 1)
    constants[2].wait()
    constants[3].wait()
    own = pltpu.make_async_copy(pieces.at[group], landed.at[group], recv_sem.at[0])

    def finish(i, carry):
        to_shard = lax.rem(shard + i, nt)
        for sub in range(4):
            k1 = to_shard * 4 + sub
            j = jnp.minimum(k1, SLOW - k1)
            real, imag = y[2 * j], y[2 * j + 1]
            cos, sin, signed_cos, signed_sin = (table[n, pl.ds(k1, 1), :] for n in range(4))
            zr = real * cos + imag * signed_sin
            zi = imag * signed_cos - real * sin
            zh, zl = split(jnp.concatenate([zr, zi], axis=1))
            both = dot_t(w2[...], zh)
            result = both[:FAST] + both[FAST:] + dot_t(w2[:FAST], zl)
            for part in range(2):
                spectrum[pl.ds(part * 4 + sub, 64, stride=8), :] = result[part * 64 : (part + 1) * 64]
        base = pl.multiple_of(i * groups, groups)
        pieces[pl.ds(base, groups)] = spectrum[...].reshape(groups, 8, FAST).astype(BF16)

        def send(dz, dx):
            to_group = lax.rem(z + dz, nz) * nx + lax.rem(x + dx, nx)
            pltpu.make_async_remote_copy(
                src_ref=pieces.at[base + to_group],
                dst_ref=landed.at[base + group],
                send_sem=send_sem,
                recv_sem=recv_sem.at[i],
                device_id={"chan": to_group, "tm": to_shard},
            ).start()

        def column(dx, inner):
            for dz in near:
                if dz:
                    send(dz, dx)
                else:

                    @pl.when(i + dx > 0)
                    def _():
                        send(0, dx)

                    @pl.when(i + dx == 0)
                    def _():
                        own.start()

            return inner

        lax.fori_loop(0, nx, column, 0)
        return carry

    lax.fori_loop(0, nt, finish, 0)

    row = lax.broadcasted_iota(jnp.int32, (channels, FAST), 0)
    counted = jnp.zeros((channels, FAST), jnp.int32)
    for channel in range(channels):
        counted = jnp.where(row == channel, counted_ref[channel], counted)
    found = []
    for slot in range(slots):
        wanted = chosen_ref[:, slot : slot + 1]
        residue = jnp.zeros((channels, FAST), F32)
        for direction in range(steering_ref.shape[0]):
            residue = jnp.where(wanted == direction, steering_ref[direction : direction + 1, :], residue)
        residue = jnp.where(counted > slot, residue, 0.0)
        for earlier in found:
            residue = residue - earlier * jnp.sum(earlier * residue, axis=-1, keepdims=True)
        found.append(residue / jnp.sqrt(jnp.sum(residue * residue, axis=-1, keepdims=True) + EPSILON))
    identity = (
        lax.broadcasted_iota(jnp.int32, (FAST, FAST), 0) == lax.broadcasted_iota(jnp.int32, (FAST, FAST), 1)
    ).astype(F32)
    for channel in range(channels):
        basis = jnp.concatenate([vector[channel : channel + 1, :] for vector in found], axis=0)
        keep_ref[channel] = identity - lax.dot_general(
            basis, basis, (((0,), (0,)), ((), ())), precision=HIGHEST, preferred_element_type=F32
        )

    gram_ref[...] = jnp.zeros(gram_ref.shape, F32)
    lower = lax.broadcasted_iota(jnp.int32, (groups, FAST), 1) < frames

    def gather(pair):
        for which in range(2):
            part = landed.at[pl.ds((2 * pair + which) * groups, groups)]
            pltpu.make_async_copy(part, part, recv_sem.at[2 * pair + which]).wait()
            wide[which * 8 * groups : (which + 1) * 8 * groups, :] = part[...].astype(F32).reshape(8 * groups, FAST)
        for channel in range(channels):
            for half in range(2):
                first = wide[pl.ds(half * 4 + channel, groups, stride=8), :]
                second = wide[pl.ds(8 * groups + half * 4 + channel, groups, stride=8), :]
                sides[channel, pl.ds(half * FAST, groups, stride=2), :] = jnp.where(
                    lower, first, pltpu.roll(second, frames, 1)
                )
                sides[channel, pl.ds(half * FAST + 1, groups, stride=2), :] = jnp.where(
                    lower, pltpu.roll(first, frames, 1), second
                )
            side = sides[channel].astype(BF16)
            outer = dot_t(side, side)
            gram_ref[channel, :FAST] += outer[:FAST, :FAST] + outer[FAST:, FAST:]
            gram_ref[channel, FAST:] += outer[FAST:, :FAST] - outer[:FAST, FAST:]

    def early(pair, carry):
        gather(pair)
        return carry

    lax.fori_loop(0, nt // 2 - 1, early, 0)
    others = pl.ds(0, nt * groups - 1)
    pltpu.make_async_copy(pieces.at[others], pieces.at[others], send_sem).wait()
    gather(nt // 2 - 1)
    copies = []
    for channel in range(channels):
        keep = keep_ref[channel]
        left = jnp.dot(gram_ref[channel], keep, precision=HIGHEST, preferred_element_type=F32)
        both = jnp.concatenate([left[:FAST], left[FAST:]], axis=1)
        result = jnp.dot(keep, both, precision=HIGHEST, preferred_element_type=F32) * (1.0 / (frames * nt))
        done[channel, 0] = result[:, :FAST]
        done[channel, 1] = result[:, FAST:]
        copies.append(pltpu.make_async_copy(done.at[channel], out_ref.at[channel], out_sem.at[channel]))
        copies[-1].start()
    for copy in copies:
        copy.wait()


def covariance(now, taps, steering, chosen, counted):
    extents = (16, 4, 4, 2)
    near = [8]
    for d in range(1, 8):
        near += [d, 16 - d]
    near.append(0)

    def kernel(*refs):
        covariance_kernel(extents, near, *refs)

    frames, rows, _ = now.shape
    tap_count, length = taps.shape
    channels = chosen.shape[0]
    w1 = np.concatenate(first_stage_matrix(), axis=0)
    w2 = second_stage_matrix()
    table = twiddles()
    vmem = pl.BlockSpec(memory_space=pltpu.VMEM)
    hbm = pl.BlockSpec(memory_space=pltpu.HBM)
    smem = pl.BlockSpec(memory_space=pltpu.SMEM)
    dma = pltpu.SemaphoreType.DMA
    return pl.pallas_call(
        kernel,
        out_shape=jax.ShapeDtypeStruct((channels, 2, FAST, FAST), F32),
        in_specs=[hbm, hbm, hbm, hbm, hbm, vmem, vmem, smem],
        out_specs=hbm,
        scratch_shapes=[
            pltpu.VMEM((frames + tap_count - 1, rows, FAST), BF16),
            pltpu.VMEM((frames + tap_count - 1, rows, FAST), F32),
            pltpu.VMEM((tap_count, length), F32),
            pltpu.VMEM((tap_count * rows, FAST), F32),
            pltpu.VMEM((2, 8, rows, FAST), F32),
            pltpu.VMEM((SLOW + 2, 2 * frames, FAST), F32),
            pltpu.VMEM((512, FAST), F32),
            pltpu.VMEM((512, 8, FAST), BF16),
            pltpu.VMEM((512, 8, FAST), BF16),
            pltpu.VMEM((1024, FAST), F32),
            pltpu.VMEM((channels, 2 * FAST, FAST), F32),
            pltpu.VMEM((channels, 2 * FAST, FAST), F32),
            pltpu.VMEM((channels, FAST, FAST), F32),
            pltpu.VMEM((channels, 2, FAST, FAST), F32),
            pltpu.VMEM(w1.shape, BF16),
            pltpu.VMEM(w2.shape, BF16),
            pltpu.VMEM(table.shape, F32),
            dma((frames // 16,)),
            dma((4,)),
            dma,
            dma,
            dma,
            dma((8,)),
            pltpu.SemaphoreType.REGULAR,
            pltpu.SemaphoreType.REGULAR,
            dma((channels,)),
        ],
        compiler_params=pltpu.CompilerParams(collective_id=0, has_side_effects=True, vmem_limit_bytes=60 << 20),
        cost_estimate=pl.CostEstimate(flops=10**9, bytes_accessed=4 << 20, transcendentals=0),
    )(now, taps, jnp.asarray(w1), jnp.asarray(w2), jnp.asarray(table), steering, chosen, counted)


def per_device(samples, taps, steering, interferer_ids, ranks):
    antennas, width = samples.shape
    length = taps.shape[1]
    frames = width // length
    blocks = samples.reshape(antennas, frames * SLOW, FAST).transpose(1, 0, 2).reshape(frames, SLOW * antennas, FAST)
    return covariance(blocks, taps, steering, interferer_ids, ranks)


def solution(mesh):
    in_specs = (P("chan", "tm"), P(), P(), P(("chan", "tm"), None), P(("chan", "tm")))
    out_specs = P(("chan", "tm"), None, None, None)
    return jax.shard_map(per_device, mesh=mesh, in_specs=in_specs, out_specs=out_specs, check_vma=False)
```

time: 85.2 us -> 78.5 us (0.921)
  Pallas kernels: 81.9 us -> 76.4 us
  local copies, waits for them, and re-layouts: 3.07 us -> 1.87 us
    pallas_call x2 -> x1, Pallas kernels: 81.9 us -> 76.4 us  [covariance(): pl.pallas_call(kernel, out_shape=jax.ShapeDtypeStruct((channels, 2, FAST,...]
    unnamed x13 -> x1, local copies, waits for them, and re-layouts: 2.29 us -> 1.87 us
where the time goes in v2:
time: 78.5 us; the launch traced here: 78.3 us
  Pallas kernels  76.4 us (97%)
  local copies, waits for them, and re-layouts  1.87 us (2%)
    pallas_call x1, Pallas kernels, covariance(): pl.pallas_call(kernel, out_shape=jax.ShapeDtypeStruct((channels, 2, FAST,...  76.4 us
    unnamed x1, local copies, waits for them, and re-layouts  1.87 us

profile of v2, /device:TPU:1, one launch (start us, length us, event | category | flops | bytes accessed | tf_op | source)
XLA Modules:
  0.0 78.3 jit_solution(16391809476059938244)
XLA Ops:
  0.0 76.4 %shard_map.82 = f32[4,2,128,128]{3,2,1,0:T(8,128)} custom-call(bf16[64,64,128]{2,1,0:T(8,128)(2,1)} %bitcast.5, f32[16,4096]{1,0:T(8,128)} %refs_1_.1, bf16[544,256]{1,0:T(8,128)(2,1)} %constant.6.clone.refs_2_, bf16[256,256]{1,0:T(8,128)(2,1)} %constant.7.clone.refs_3_, f32[4,32,128]{2,1,0:T(8,128)} %constant.8.clone.refs_4_, f32[8,128]{1,0:T(8,128)} %refs_5_.1, ...), custom_call_target="tpu_custom_call" | custom-call | flops 1000000000 | bytes 4194304 | tf_op jit(solution)/shard_map/pallas_call | solution.py:341
  76.5 1.9 %copy.11 = f32[4,2,128,128]{3,2,1,0:T(8,128)} copy(f32[4,2,128,128]{3,2,1,0:T(8,128)} %shard_map.82) | data formatting | bytes 1048576

commit v3 on v2

--- a/solution.py
+++ b/solution.py
@@ -61,9 +61,9 @@
 
 
 def covariance_kernel(extents, near, now_ref, taps_ref, w1_ref, w2_ref, table_ref, steering_ref, chosen_ref, counted_ref,
-                      out_ref, arrived, window, taps, weights, filtered, y, spectrum, pieces, landed, wide, sides,
+                      out_ref, arrived, window, taps, weights, even, odd, y, spectrum, pieces, landed, wide, sides,
                       gram_ref, keep_ref, done, w1, w2, table, in_sem, const_sem, halo_send, halo_recv, send_sem, recv_sem,
-                      line_sem, whole_sem, out_sem):
+                      plane_sem, whole_sem, out_sem):
     nz, nx, ny, nc = extents
     nt = ny * nc
     groups = nz * nx
@@ -96,7 +96,9 @@
         copy.start()
 
     barrier = pltpu.get_barrier_semaphore()
-    for count, line in ((nz, along_z), (nt, along_t), (nx, along_x)):
+    for d in near[:-1]:
+        pl.semaphore_signal(barrier, inc=1, device_id=along_z(d))
+    for count, line in ((nt, along_t), (nx, along_x)):
         for d in range(1, count):
             pl.semaphore_signal(barrier, inc=1, device_id=line(d))
 
@@ -111,17 +113,15 @@
             for a in range(2):
                 weights[pl.ds(t * rows + 2 * p + a, 8, stride=rows), :] = tile
 
-    def widen(i):
-        inputs[i].wait()
-
-        def convert(g, carry):
-            at = halo + i * 16 + g * 8
-            window[pl.ds(at, 8)] = arrived[pl.ds(at, 8)].astype(F32)
-            return carry
-
-        lax.fori_loop(0, 2, convert, 0)
-
-    def filter_group(g):
+    def widen(first, last):
+        window[first:last] = arrived[first:last].astype(F32)
+
+    def widen_group(g):
+        if g % 2 == 0:
+            inputs[g // 2].wait()
+        widen(halo + g * 8, halo + g * 8 + 8)
+
+    def filter_group(g, filtered):
         for r in range(0, rows, 8):
             tap = [weights[t * rows + r : t * rows + r + 8, :] for t in range(tap_count)]
             seen = [window[g * 8 + i, r : r + 8, :] for i in range(8 + halo)]
@@ -129,12 +129,12 @@
                 result = tap[0] * seen[f]
                 for t in range(1, tap_count):
                     result = result + tap[t] * seen[f + t]
-                filtered[g % 2, f, r : r + 8, :] = result
-
-    def turn_group(g):
+                filtered[f, r : r + 8, :] = result
+
+    def turn_group(g, filtered):
         columns_h, columns_l = [], []
         for a in range(2):
-            parts = [split(filtered[g % 2, f, pl.ds(a, SLOW, stride=2), :]) for f in range(8)]
+            parts = [split(filtered[f, pl.ds(a, SLOW, stride=2), :]) for f in range(8)]
             columns_h.append(jnp.concatenate([h for h, _ in parts], axis=0))
             columns_l.append(jnp.concatenate([l for _, l in parts], axis=0))
         xh = jnp.concatenate(columns_h, axis=1)
@@ -146,63 +146,60 @@
             piece = turned[:, a * FAST : (a + 1) * FAST].reshape(SLOW + 2, 8, FAST)
             y[:, a * frames + g * 8 : a * frames + g * 8 + 8, :] = piece
 
-    widen(0)
-    widen(1)
-    filter_group(2)
+    for g in range(3):
+        widen_group(g)
+    filter_group(2, even)
     constants[1].wait()
-    widen(2)
-    filter_group(3)
-    turn_group(2)
-    widen(3)
+    widen_group(3)
+    filter_group(3, odd)
+    turn_group(2, even)
 
     pl.semaphore_wait(barrier, nz + nx + nt - 3)
-    carried = pltpu.make_async_remote_copy(
-        src_ref=now_ref.at[pl.ds(frames - halo, halo)],
-        dst_ref=arrived.at[pl.ds(0, halo)],
-        send_sem=halo_send,
-        recv_sem=halo_recv,
-        device_id=along_t(1),
-    )
+    near_halo = halo // 2
+    carried = [
+        pltpu.make_async_remote_copy(
+            src_ref=now_ref.at[pl.ds(frames - halo + first, count)],
+            dst_ref=arrived.at[pl.ds(first, count)],
+            send_sem=halo_send.at[i],
+            recv_sem=halo_recv.at[i],
+            device_id=along_t(1),
+        )
+        for i, (first, count) in enumerate(((halo - near_halo, near_halo), (0, halo - near_halo)))
+    ]
 
     @pl.when(shard < nt - 1)
     def _():
-        carried.start()
-
-    for d in range(1, nt):
-        pl.semaphore_signal(line_sem, inc=1, device_id=along_t(d))
-
-    filter_group(4)
-    turn_group(3)
-    filter_group(5)
-    turn_group(4)
-    pl.semaphore_wait(line_sem, nt - 1)
+        for copy in carried:
+            copy.start()
+
     for d in range(1, nx):
-        pl.semaphore_signal(whole_sem, inc=1, device_id=along_x(d))
-    filter_group(6)
-    turn_group(5)
-    filter_group(7)
-    turn_group(6)
+        pl.semaphore_signal(plane_sem, inc=1, device_id=along_x(d))
+
+    for g in range(4, 8):
+        widen_group(g)
+        filter_group(g, odd if g % 2 else even)
+        turn_group(g - 1, even if g % 2 else odd)
 
     @pl.when(shard > 0)
     def _():
-        carried.wait_recv()
-
-    @pl.when(shard < nt - 1)
+        carried[0].wait_recv()
+
+    widen(halo - near_halo, halo)
+    filter_group(1, even)
+    turn_group(7, odd)
+
+    @pl.when(shard > 0)
     def _():
-        carried.wait_send()
-
-    window[0:halo] = arrived[0:halo].astype(F32)
-    filter_group(0)
-    turn_group(7)
-    filter_group(1)
-    turn_group(0)
-    turn_group(1)
-    pl.semaphore_wait(whole_sem, nx - 1)
+        carried[1].wait_recv()
+
+    widen(0, halo - near_halo)
+    filter_group(0, odd)
+    turn_group(1, even)
+    turn_group(0, odd)
     constants[2].wait()
     constants[3].wait()
-    own = pltpu.make_async_copy(pieces.at[group], landed.at[group], recv_sem.at[0])
-
-    def finish(i, carry):
+
+    def finish(i):
         to_shard = lax.rem(shard + i, nt)
         for sub in range(4):
             k1 = to_shard * 4 + sub
@@ -219,36 +216,42 @@
         base = pl.multiple_of(i * groups, groups)
         pieces[pl.ds(base, groups)] = spectrum[...].reshape(groups, 8, FAST).astype(BF16)
 
-        def send(dz, dx):
-            to_group = lax.rem(z + dz, nz) * nx + lax.rem(x + dx, nx)
-            pltpu.make_async_remote_copy(
-                src_ref=pieces.at[base + to_group],
-                dst_ref=landed.at[base + group],
-                send_sem=send_sem,
-                recv_sem=recv_sem.at[i],
-                device_id={"chan": to_group, "tm": to_shard},
-            ).start()
-
-        def column(dx, inner):
+    def send(i, dz, dx):
+        to_shard = lax.rem(shard + i, nt)
+        to_group = lax.rem(z + dz, nz) * nx + lax.rem(x + dx, nx)
+        pltpu.make_async_remote_copy(
+            src_ref=pieces.at[i * groups + to_group],
+            dst_ref=landed.at[i * groups + group],
+            send_sem=send_sem,
+            recv_sem=recv_sem.at[i],
+            device_id={"chan": to_group, "tm": to_shard},
+        ).start()
+
+    def columns(i, first):
+        def column(dx, carry):
             for dz in near:
-                if dz:
-                    send(dz, dx)
-                else:
-
-                    @pl.when(i + dx > 0)
-                    def _():
-                        send(0, dx)
-
-                    @pl.when(i + dx == 0)
-                    def _():
-                        own.start()
-
-            return inner
-
-        lax.fori_loop(0, nx, column, 0)
+                send(i, dz, dx)
+            return carry
+
+        lax.fori_loop(first, nx, column, 0)
+
+    zero = jnp.int32(0)
+    finish(zero)
+    for dz in near[:-1]:
+        send(zero, dz, 0)
+    pltpu.make_async_copy(pieces.at[group], landed.at[group], recv_sem.at[0]).start()
+    pl.semaphore_wait(plane_sem, nx - 1)
+    for d in range(1, nt):
+        pl.semaphore_signal(whole_sem, inc=1, device_id=along_t(d))
+    columns(zero, 1)
+    pl.semaphore_wait(whole_sem, nt - 1)
+
+    def onward(i, carry):
+        finish(i)
+        columns(i, 0)
         return carry
 
-    lax.fori_loop(0, nt, finish, 0)
+    lax.fori_loop(1, nt, onward, 0)
 
     row = lax.broadcasted_iota(jnp.int32, (channels, FAST), 0)
     counted = jnp.zeros((channels, FAST), jnp.int32)
@@ -269,9 +272,10 @@
     ).astype(F32)
     for channel in range(channels):
         basis = jnp.concatenate([vector[channel : channel + 1, :] for vector in found], axis=0)
-        keep_ref[channel] = identity - lax.dot_general(
+        keep = identity - lax.dot_general(
             basis, basis, (((0,), (0,)), ((), ())), precision=HIGHEST, preferred_element_type=F32
         )
+        keep_ref[channel, :FAST], keep_ref[channel, FAST:] = split(keep)
 
     gram_ref[...] = jnp.zeros(gram_ref.shape, F32)
     lower = lax.broadcasted_iota(jnp.int32, (groups, FAST), 1) < frames
@@ -303,13 +307,20 @@
     lax.fori_loop(0, nt // 2 - 1, early, 0)
     others = pl.ds(0, nt * groups - 1)
     pltpu.make_async_copy(pieces.at[others], pieces.at[others], send_sem).wait()
+
+    @pl.when(shard < nt - 1)
+    def _():
+        for copy in carried:
+            copy.wait_send()
+
     gather(nt // 2 - 1)
     copies = []
     for channel in range(channels):
-        keep = keep_ref[channel]
-        left = jnp.dot(gram_ref[channel], keep, precision=HIGHEST, preferred_element_type=F32)
-        both = jnp.concatenate([left[:FAST], left[FAST:]], axis=1)
-        result = jnp.dot(keep, both, precision=HIGHEST, preferred_element_type=F32) * (1.0 / (frames * nt))
+        keep_h, keep_l = keep_ref[channel, :FAST], keep_ref[channel, FAST:]
+        gram_h, gram_l = split(gram_ref[channel])
+        left = dot(gram_h, keep_h) + dot(gram_l, keep_h) + dot(gram_h, keep_l)
+        left_h, left_l = split(jnp.concatenate([left[:FAST], left[FAST:]], axis=1))
+        result = (dot(keep_h, left_h) + dot(keep_h, left_l) + dot(keep_l, left_h)) * (1.0 / (frames * nt))
         done[channel, 0] = result[:, :FAST]
         done[channel, 1] = result[:, FAST:]
         copies.append(pltpu.make_async_copy(done.at[channel], out_ref.at[channel], out_sem.at[channel]))
@@ -321,7 +332,7 @@
 def covariance(now, taps, steering, chosen, counted):
     extents = (16, 4, 4, 2)
     near = [8]
-    for d in range(1, 8):
+    for d in range(7, 0, -1):
         near += [d, 16 - d]
     near.append(0)
 
@@ -348,7 +359,8 @@
             pltpu.VMEM((frames + tap_count - 1, rows, FAST), F32),
             pltpu.VMEM((tap_count, length), F32),
             pltpu.VMEM((tap_count * rows, FAST), F32),
-            pltpu.VMEM((2, 8, rows, FAST), F32),
+            pltpu.VMEM((8, rows, FAST), F32),
+            pltpu.VMEM((8, rows, FAST), F32),
             pltpu.VMEM((SLOW + 2, 2 * frames, FAST), F32),
             pltpu.VMEM((512, FAST), F32),
             pltpu.VMEM((512, 8, FAST), BF16),
@@ -356,15 +368,15 @@
             pltpu.VMEM((1024, FAST), F32),
             pltpu.VMEM((channels, 2 * FAST, FAST), F32),
             pltpu.VMEM((channels, 2 * FAST, FAST), F32),
-            pltpu.VMEM((channels, FAST, FAST), F32),
+            pltpu.VMEM((channels, 2 * FAST, FAST), BF16),
             pltpu.VMEM((channels, 2, FAST, FAST), F32),
             pltpu.VMEM(w1.shape, BF16),
             pltpu.VMEM(w2.shape, BF16),
             pltpu.VMEM(table.shape, F32),
             dma((frames // 16,)),
             dma((4,)),
-            dma,
-            dma,
+            dma((2,)),
+            dma((2,)),
             dma,
             dma((8,)),
             pltpu.SemaphoreType.REGULAR,

time: 78.5 us -> 76.2 us (0.971)
  Pallas kernels: 76.4 us -> 74.1 us
    pallas_call x1, Pallas kernels: 76.4 us -> 74.1 us  [covariance(): pl.pallas_call(kernel, out_shape=jax.ShapeDtypeStruct((channels, 2, FAST,...]
where the time goes in v3:
time: 76.2 us; the launch traced here: 76 us
  Pallas kernels  74.1 us (97%)
  local copies, waits for them, and re-layouts  1.87 us (2%)
    pallas_call x1, Pallas kernels, covariance(): pl.pallas_call(kernel, out_shape=jax.ShapeDtypeStruct((channels, 2, FAST,...  74.1 us
    unnamed x1, local copies, waits for them, and re-layouts  1.87 us

profile of v3, /device:TPU:1, one launch (start us, length us, event | category | flops | bytes accessed | tf_op | source)
XLA Modules:
  0.0 76.0 jit_solution(13202881232749765823)
XLA Ops:
  0.0 74.1 %shard_map.82 = f32[4,2,128,128]{3,2,1,0:T(8,128)} custom-call(bf16[64,64,128]{2,1,0:T(8,128)(2,1)} %bitcast.5, f32[16,4096]{1,0:T(8,128)} %refs_1_.1, bf16[544,256]{1,0:T(8,128)(2,1)} %constant.6.clone.refs_2_, bf16[256,256]{1,0:T(8,128)(2,1)} %constant.7.clone.refs_3_, f32[4,32,128]{2,1,0:T(8,128)} %constant.8.clone.refs_4_, f32[8,128]{1,0:T(8,128)} %refs_5_.1, ...), custom_call_target="tpu_custom_call" | custom-call | flops 1000000000 | bytes 4194304 | tf_op jit(solution)/shard_map/pallas_call | solution.py:352
  74.1 1.9 %copy.11 = f32[4,2,128,128]{3,2,1,0:T(8,128)} copy(f32[4,2,128,128]{3,2,1,0:T(8,128)} %shard_map.82) | data formatting | bytes 1048576

commit v4 on v3

--- a/solution.py
+++ b/solution.py
@@ -37,8 +37,7 @@
     angle = 2.0 * np.pi * turns / FAST
     real_rows = np.concatenate([np.cos(angle), np.sin(angle)], axis=1)
     imag_rows = np.concatenate([-np.sin(angle), np.cos(angle)], axis=1)
-    high, low = split_constant(np.concatenate([real_rows, imag_rows], axis=0))
-    return np.concatenate([high, low], axis=0)
+    return split_constant(np.concatenate([real_rows, imag_rows], axis=0))
 
 
 def twiddles():
@@ -52,6 +51,10 @@
     return high, (values - high.astype(F32)).astype(BF16)
 
 
+def beside(high, low, axis):
+    return jnp.concatenate([high, low, high], axis=axis)
+
+
 def dot(a, b):
     return lax.dot_general(a, b, (((1,), (0,)), ((), ())), preferred_element_type=F32)
 
@@ -62,8 +65,8 @@
 
 def covariance_kernel(extents, near, now_ref, taps_ref, w1_ref, w2_ref, table_ref, steering_ref, chosen_ref, counted_ref,
                       out_ref, arrived, window, taps, weights, even, odd, y, spectrum, pieces, landed, wide, sides,
-                      gram_ref, keep_ref, done, w1, w2, table, in_sem, const_sem, halo_send, halo_recv, send_sem, recv_sem,
-                      plane_sem, whole_sem, out_sem):
+                      gram_ref, below, aside, steering, chosen, counted_scalar, w1, w2, table, in_sem, const_sem, halo_send, halo_recv, send_sem, recv_sem,
+                      plane_sem, whole_sem):
     nz, nx, ny, nc = extents
     nt = ny * nc
     groups = nz * nx
@@ -84,9 +87,18 @@
     def along_t(d):
         return {"tm": lax.rem(shard + d, nt)}
 
+    pairs = (
+        (taps_ref, taps),
+        (w1_ref, w1),
+        (w2_ref, w2),
+        (table_ref, table),
+        (steering_ref, steering),
+        (chosen_ref, chosen),
+        (counted_ref, counted_scalar),
+    )
     constants = [
         pltpu.make_async_copy(source, target, const_sem.at[i])
-        for i, (source, target) in enumerate(((taps_ref, taps), (w1_ref, w1), (w2_ref, w2), (table_ref, table)))
+        for i, (source, target) in enumerate(pairs)
     ]
     inputs = [
         pltpu.make_async_copy(now_ref.at[pl.ds(i * 16, 16)], arrived.at[pl.ds(halo + i * 16, 16)], in_sem.at[i])
@@ -139,9 +151,7 @@
             columns_l.append(jnp.concatenate([l for _, l in parts], axis=0))
         xh = jnp.concatenate(columns_h, axis=1)
         xl = jnp.concatenate(columns_l, axis=1)
-        size = (SLOW + 2) * 8
-        both = dot(w1[...], xh)
-        turned = both[:size] + both[size:] + dot(w1[:size], xl)
+        turned = dot(w1[...], jnp.concatenate([xh, xh, xl], axis=0))
         for a in range(2):
             piece = turned[:, a * FAST : (a + 1) * FAST].reshape(SLOW + 2, 8, FAST)
             y[:, a * frames + g * 8 : a * frames + g * 8 + 8, :] = piece
@@ -196,8 +206,8 @@
     filter_group(0, odd)
     turn_group(1, even)
     turn_group(0, odd)
-    constants[2].wait()
-    constants[3].wait()
+    for copy in constants[2:]:
+        copy.wait()
 
     def finish(i):
         to_shard = lax.rem(shard + i, nt)
@@ -209,8 +219,7 @@
             zr = real * cos + imag * signed_sin
             zi = imag * signed_cos - real * sin
             zh, zl = split(jnp.concatenate([zr, zi], axis=1))
-            both = dot_t(w2[...], zh)
-            result = both[:FAST] + both[FAST:] + dot_t(w2[:FAST], zl)
+            result = dot_t(w2[...], jnp.concatenate([zh, zh, zl], axis=1))
             for part in range(2):
                 spectrum[pl.ds(part * 4 + sub, 64, stride=8), :] = result[part * 64 : (part + 1) * 64]
         base = pl.multiple_of(i * groups, groups)
@@ -242,12 +251,12 @@
     pltpu.make_async_copy(pieces.at[group], landed.at[group], recv_sem.at[0]).start()
     pl.semaphore_wait(plane_sem, nx - 1)
     for d in range(1, nt):
-        pl.semaphore_signal(whole_sem, inc=1, device_id=along_t(d))
+        pl.semaphore_signal(whole_sem.at[nt - d], inc=1, device_id=along_t(d))
     columns(zero, 1)
-    pl.semaphore_wait(whole_sem, nt - 1)
 
     def onward(i, carry):
         finish(i)
+        pl.semaphore_wait(whole_sem.at[i], 1)
         columns(i, 0)
         return carry
 
@@ -256,13 +265,13 @@
     row = lax.broadcasted_iota(jnp.int32, (channels, FAST), 0)
     counted = jnp.zeros((channels, FAST), jnp.int32)
     for channel in range(channels):
-        counted = jnp.where(row == channel, counted_ref[channel], counted)
+        counted = jnp.where(row == channel, counted_scalar[channel], counted)
     found = []
     for slot in range(slots):
-        wanted = chosen_ref[:, slot : slot + 1]
+        wanted = chosen[:, slot : slot + 1]
         residue = jnp.zeros((channels, FAST), F32)
-        for direction in range(steering_ref.shape[0]):
-            residue = jnp.where(wanted == direction, steering_ref[direction : direction + 1, :], residue)
+        for direction in range(steering.shape[0]):
+            residue = jnp.where(wanted == direction, steering[direction : direction + 1, :], residue)
         residue = jnp.where(counted > slot, residue, 0.0)
         for earlier in found:
             residue = residue - earlier * jnp.sum(earlier * residue, axis=-1, keepdims=True)
@@ -275,12 +284,14 @@
         keep = identity - lax.dot_general(
             basis, basis, (((0,), (0,)), ((), ())), precision=HIGHEST, preferred_element_type=F32
         )
-        keep_ref[channel, :FAST], keep_ref[channel, FAST:] = split(keep)
+        keep_h, keep_l = split(keep)
+        below[channel] = beside(keep_h, keep_l, 0)
+        aside[channel] = beside(keep_h, keep_l, 1)
 
     gram_ref[...] = jnp.zeros(gram_ref.shape, F32)
     lower = lax.broadcasted_iota(jnp.int32, (groups, FAST), 1) < frames
 
-    def gather(pair):
+    def gather(pair, use):
         for which in range(2):
             part = landed.at[pl.ds((2 * pair + which) * groups, groups)]
             pltpu.make_async_copy(part, part, recv_sem.at[2 * pair + which]).wait()
@@ -297,11 +308,15 @@
                 )
             side = sides[channel].astype(BF16)
             outer = dot_t(side, side)
-            gram_ref[channel, :FAST] += outer[:FAST, :FAST] + outer[FAST:, FAST:]
-            gram_ref[channel, FAST:] += outer[FAST:, :FAST] - outer[:FAST, FAST:]
+            real = gram_ref[channel, :FAST] + (outer[:FAST, :FAST] + outer[FAST:, FAST:])
+            imag = gram_ref[channel, FAST:] + (outer[FAST:, :FAST] - outer[:FAST, FAST:])
+            use(channel, jnp.concatenate([real, imag], axis=0))
+
+    def keep_sum(channel, gram):
+        gram_ref[channel] = gram
 
     def early(pair, carry):
-        gather(pair)
+        gather(pair, keep_sum)
         return carry
 
     lax.fori_loop(0, nt // 2 - 1, early, 0)
@@ -313,20 +328,15 @@
         for copy in carried:
             copy.wait_send()
 
-    gather(nt // 2 - 1)
-    copies = []
-    for channel in range(channels):
-        keep_h, keep_l = keep_ref[channel, :FAST], keep_ref[channel, FAST:]
-        gram_h, gram_l = split(gram_ref[channel])
-        left = dot(gram_h, keep_h) + dot(gram_l, keep_h) + dot(gram_h, keep_l)
+    def project(channel, gram):
+        gram_h, gram_l = split(gram)
+        left = dot(jnp.concatenate([gram_h, gram_h, gram_l], axis=1), below[channel])
         left_h, left_l = split(jnp.concatenate([left[:FAST], left[FAST:]], axis=1))
-        result = (dot(keep_h, left_h) + dot(keep_h, left_l) + dot(keep_l, left_h)) * (1.0 / (frames * nt))
-        done[channel, 0] = result[:, :FAST]
-        done[channel, 1] = result[:, FAST:]
-        copies.append(pltpu.make_async_copy(done.at[channel], out_ref.at[channel], out_sem.at[channel]))
-        copies[-1].start()
-    for copy in copies:
-        copy.wait()
+        result = dot(aside[channel], jnp.concatenate([left_h, left_h, left_l], axis=0)) * (1.0 / (frames * nt))
+        out_ref[channel, 0] = result[:, :FAST]
+        out_ref[channel, 1] = result[:, FAST:]
+
+    gather(nt // 2 - 1, project)
 
 
 def covariance(now, taps, steering, chosen, counted):
@@ -342,18 +352,19 @@
     frames, rows, _ = now.shape
     tap_count, length = taps.shape
     channels = chosen.shape[0]
-    w1 = np.concatenate(first_stage_matrix(), axis=0)
-    w2 = second_stage_matrix()
+    w1_high, w1_low = first_stage_matrix()
+    w1 = np.concatenate([w1_high, w1_low, w1_high], axis=1)
+    w2_high, w2_low = second_stage_matrix()
+    w2 = np.concatenate([w2_high, w2_low, w2_high], axis=1)
     table = twiddles()
     vmem = pl.BlockSpec(memory_space=pltpu.VMEM)
     hbm = pl.BlockSpec(memory_space=pltpu.HBM)
-    smem = pl.BlockSpec(memory_space=pltpu.SMEM)
     dma = pltpu.SemaphoreType.DMA
     return pl.pallas_call(
         kernel,
         out_shape=jax.ShapeDtypeStruct((channels, 2, FAST, FAST), F32),
-        in_specs=[hbm, hbm, hbm, hbm, hbm, vmem, vmem, smem],
-        out_specs=hbm,
+        in_specs=[hbm] * 8,
+        out_specs=vmem,
         scratch_shapes=[
             pltpu.VMEM((frames + tap_count - 1, rows, FAST), BF16),
             pltpu.VMEM((frames + tap_count - 1, rows, FAST), F32),
@@ -368,24 +379,31 @@
             pltpu.VMEM((1024, FAST), F32),
             pltpu.VMEM((channels, 2 * FAST, FAST), F32),
             pltpu.VMEM((channels, 2 * FAST, FAST), F32),
-            pltpu.VMEM((channels, 2 * FAST, FAST), BF16),
-            pltpu.VMEM((channels, 2, FAST, FAST), F32),
+            pltpu.VMEM((channels, 3 * FAST, FAST), BF16),
+            pltpu.VMEM((channels, FAST, 3 * FAST), BF16),
+            pltpu.VMEM(steering.shape, F32),
+            pltpu.VMEM(chosen.shape, jnp.int32),
+            pltpu.SMEM(counted.shape, jnp.int32),
             pltpu.VMEM(w1.shape, BF16),
             pltpu.VMEM(w2.shape, BF16),
             pltpu.VMEM(table.shape, F32),
             dma((frames // 16,)),
-            dma((4,)),
+            dma((7,)),
             dma((2,)),
             dma((2,)),
             dma,
             dma((8,)),
             pltpu.SemaphoreType.REGULAR,
-            pltpu.SemaphoreType.REGULAR,
-            dma((channels,)),
+            pltpu.SemaphoreType.REGULAR((8,)),
         ],
-        compiler_params=pltpu.CompilerParams(collective_id=0, has_side_effects=True, vmem_limit_bytes=60 << 20),
+        compiler_params=pltpu.CompilerParams(collective_id=0, has_side_effects=True, vmem_limit_bytes=40 << 20),
         cost_estimate=pl.CostEstimate(flops=10**9, bytes_accessed=4 << 20, transcendentals=0),
-    )(now, taps, jnp.asarray(w1), jnp.asarray(w2), jnp.asarray(table), steering, chosen, counted)
+    )(
+        *(
+            pltpu.with_memory_space_constraint(value, pltpu.HBM)
+            for value in (now, taps, jnp.asarray(w1), jnp.asarray(w2), jnp.asarray(table), steering, chosen, counted)
+        )
+    )
 
 
 def per_device(samples, taps, steering, interferer_ids, ranks):

time: 76.2 us -> 74 us (0.971)
  local copies, waits for them, and re-layouts: 1.87 us -> 0.8 us
  Pallas kernels: 74.1 us -> 73.1 us
    unnamed x1, local copies, waits for them, and re-layouts: 1.87 us -> 0.8 us
    pallas_call x1, Pallas kernels: 74.1 us -> 73.1 us  [covariance(): pl.pallas_call(kernel, out_shape=jax.ShapeDtypeStruct((channels, 2, FAST,...]
where the time goes in v4:
time: 74 us; the launch traced here: 73.9 us
  Pallas kernels  73.1 us (99%)
  local copies, waits for them, and re-layouts  0.8 us (1%)
    pallas_call x1, Pallas kernels, covariance(): pl.pallas_call(kernel, out_shape=jax.ShapeDtypeStruct((channels, 2, FAST,...  73.1 us

profile of v4, /device:TPU:1, one launch (start us, length us, event | category | flops | bytes accessed | tf_op | source)
XLA Modules:
  0.0 73.9 jit_solution(18051086959682351835)
XLA Ops:
  0.0 73.1 %shard_map.82 = f32[4,2,128,128]{3,2,1,0:T(8,128)S(1)} custom-call(bf16[64,64,128]{2,1,0:T(8,128)(2,1)} %bitcast.5, f32[16,4096]{1,0:T(8,128)} %refs_1_.1, bf16[272,768]{1,0:T(8,128)(2,1)} %constant.6.clone.refs_2_, bf16[128,768]{1,0:T(8,128)(2,1)} %constant.7.clone.refs_3_, f32[4,32,128]{2,1,0:T(8,128)} %constant.8.clone.refs_4_, f32[8,128]{1,0:T(8,128)} %refs_5_.1, ...), custom_call_target="tpu_custom_call" | custom-call | flops 1000000000 | bytes 4194304 | tf_op jit(solution)/shard_map/pallas_call | solution.py:363
  73.1 0.8 %copy.11 = f32[4,2,128,128]{3,2,1,0:T(8,128)} copy(f32[4,2,128,128]{3,2,1,0:T(8,128)S(1)} %shard_map.82) | data formatting | bytes 1048576

commit v5 on v4

--- a/solution.py
+++ b/solution.py
@@ -64,7 +64,7 @@
 
 
 def covariance_kernel(extents, near, now_ref, taps_ref, w1_ref, w2_ref, table_ref, steering_ref, chosen_ref, counted_ref,
-                      out_ref, arrived, window, taps, weights, even, odd, y, spectrum, pieces, landed, wide, sides,
+                      out_ref, arrived, window, taps, weights, early_part, late_part, y, spectrum, pieces, landed, wide, sides,
                       gram_ref, below, aside, steering, chosen, counted_scalar, w1, w2, table, in_sem, const_sem, halo_send, halo_recv, send_sem, recv_sem,
                       plane_sem, whole_sem):
     nz, nx, ny, nc = extents
@@ -133,7 +133,7 @@
             inputs[g // 2].wait()
         widen(halo + g * 8, halo + g * 8 + 8)
 
-    def filter_group(g, filtered):
+    def filter_group(g, filtered, place):
         for r in range(0, rows, 8):
             tap = [weights[t * rows + r : t * rows + r + 8, :] for t in range(tap_count)]
             seen = [window[g * 8 + i, r : r + 8, :] for i in range(8 + halo)]
@@ -141,28 +141,30 @@
                 result = tap[0] * seen[f]
                 for t in range(1, tap_count):
                     result = result + tap[t] * seen[f + t]
-                filtered[f, r : r + 8, :] = result
-
-    def turn_group(g, filtered):
+                filtered[place * 8 + f, r : r + 8, :] = result
+
+    def turn_groups(order, filtered):
         columns_h, columns_l = [], []
-        for a in range(2):
-            parts = [split(filtered[f, pl.ds(a, SLOW, stride=2), :]) for f in range(8)]
-            columns_h.append(jnp.concatenate([h for h, _ in parts], axis=0))
-            columns_l.append(jnp.concatenate([l for _, l in parts], axis=0))
+        for place in range(len(order)):
+            for a in range(2):
+                parts = [split(filtered[place * 8 + f, pl.ds(a, SLOW, stride=2), :]) for f in range(8)]
+                columns_h.append(jnp.concatenate([h for h, _ in parts], axis=0))
+                columns_l.append(jnp.concatenate([l for _, l in parts], axis=0))
         xh = jnp.concatenate(columns_h, axis=1)
         xl = jnp.concatenate(columns_l, axis=1)
         turned = dot(w1[...], jnp.concatenate([xh, xh, xl], axis=0))
-        for a in range(2):
-            piece = turned[:, a * FAST : (a + 1) * FAST].reshape(SLOW + 2, 8, FAST)
-            y[:, a * frames + g * 8 : a * frames + g * 8 + 8, :] = piece
+        for place, g in enumerate(order):
+            for a in range(2):
+                at = (2 * place + a) * FAST
+                piece = turned[:, at : at + FAST].reshape(SLOW + 2, 8, FAST)
+                y[:, a * frames + g * 8 : a * frames + g * 8 + 8, :] = piece
 
     for g in range(3):
         widen_group(g)
-    filter_group(2, even)
+    filter_group(2, early_part, 0)
     constants[1].wait()
     widen_group(3)
-    filter_group(3, odd)
-    turn_group(2, even)
+    filter_group(3, early_part, 1)
 
     pl.semaphore_wait(barrier, nz + nx + nt - 3)
     near_halo = halo // 2
@@ -185,27 +187,28 @@
     for d in range(1, nx):
         pl.semaphore_signal(plane_sem, inc=1, device_id=along_x(d))
 
-    for g in range(4, 8):
+    for g in (4, 5):
         widen_group(g)
-        filter_group(g, odd if g % 2 else even)
-        turn_group(g - 1, even if g % 2 else odd)
+        filter_group(g, early_part, g - 2)
+    turn_groups((2, 3, 4, 5), early_part)
+    for g in (6, 7):
+        widen_group(g)
+        filter_group(g, late_part, g - 6)
 
     @pl.when(shard > 0)
     def _():
         carried[0].wait_recv()
 
     widen(halo - near_halo, halo)
-    filter_group(1, even)
-    turn_group(7, odd)
+    filter_group(1, late_part, 2)
 
     @pl.when(shard > 0)
     def _():
         carried[1].wait_recv()
 
     widen(0, halo - near_halo)
-    filter_group(0, odd)
-    turn_group(1, even)
-    turn_group(0, odd)
+    filter_group(0, late_part, 3)
+    turn_groups((6, 7, 1, 0), late_part)
     for copy in constants[2:]:
         copy.wait()
 
@@ -370,8 +373,8 @@
             pltpu.VMEM((frames + tap_count - 1, rows, FAST), F32),
             pltpu.VMEM((tap_count, length), F32),
             pltpu.VMEM((tap_count * rows, FAST), F32),
-            pltpu.VMEM((8, rows, FAST), F32),
-            pltpu.VMEM((8, rows, FAST), F32),
+            pltpu.VMEM((32, rows, FAST), F32),
+            pltpu.VMEM((32, rows, FAST), F32),
             pltpu.VMEM((SLOW + 2, 2 * frames, FAST), F32),
             pltpu.VMEM((512, FAST), F32),
             pltpu.VMEM((512, 8, FAST), BF16),

time: 74 us -> 72.9 us (0.985)
  Pallas kernels: 73.1 us -> 72 us
    pallas_call x1, Pallas kernels: 73.1 us -> 72 us  [covariance(): pl.pallas_call(kernel, out_shape=jax.ShapeDtypeStruct((channels, 2, FAST,...]
where the time goes in v5:
time: 72.9 us; the launch traced here: 72.8 us
  Pallas kernels  72 us (99%)
  local copies, waits for them, and re-layouts  0.8 us (1%)
    pallas_call x1, Pallas kernels, covariance(): pl.pallas_call(kernel, out_shape=jax.ShapeDtypeStruct((channels, 2, FAST,...  72 us

profile of v5, /device:TPU:1, one launch (start us, length us, event | category | flops | bytes accessed | tf_op | source)
XLA Modules:
  0.0 72.8 jit_solution(7761222029483359765)
XLA Ops:
  0.0 72.0 %shard_map.82 = f32[4,2,128,128]{3,2,1,0:T(8,128)S(1)} custom-call(bf16[64,64,128]{2,1,0:T(8,128)(2,1)} %bitcast.5, f32[16,4096]{1,0:T(8,128)} %refs_1_.1, bf16[272,768]{1,0:T(8,128)(2,1)} %constant.6.clone.refs_2_, bf16[128,768]{1,0:T(8,128)(2,1)} %constant.7.clone.refs_3_, f32[4,32,128]{2,1,0:T(8,128)} %constant.8.clone.refs_4_, f32[8,128]{1,0:T(8,128)} %refs_5_.1, ...), custom_call_target="tpu_custom_call" | custom-call | flops 1000000000 | bytes 4194304 | tf_op jit(solution)/shard_map/pallas_call | solution.py:366
  72.0 0.8 %copy.11 = f32[4,2,128,128]{3,2,1,0:T(8,128)} copy(f32[4,2,128,128]{3,2,1,0:T(8,128)S(1)} %shard_map.82) | data formatting | bytes 1048576

commit v6 on v5

--- a/solution.py
+++ b/solution.py
@@ -194,21 +194,22 @@
     for g in (6, 7):
         widen_group(g)
         filter_group(g, late_part, g - 6)
+    turn_groups((6, 7), late_part)
 
     @pl.when(shard > 0)
     def _():
         carried[0].wait_recv()
 
     widen(halo - near_halo, halo)
-    filter_group(1, late_part, 2)
+    filter_group(1, early_part, 0)
 
     @pl.when(shard > 0)
     def _():
         carried[1].wait_recv()
 
     widen(0, halo - near_halo)
-    filter_group(0, late_part, 3)
-    turn_groups((6, 7, 1, 0), late_part)
+    filter_group(0, early_part, 1)
+    turn_groups((1, 0), early_part)
     for copy in constants[2:]:
         copy.wait()
 
@@ -374,7 +375,7 @@
             pltpu.VMEM((tap_count, length), F32),
             pltpu.VMEM((tap_count * rows, FAST), F32),
             pltpu.VMEM((32, rows, FAST), F32),
-            pltpu.VMEM((32, rows, FAST), F32),
+            pltpu.VMEM((16, rows, FAST), F32),
             pltpu.VMEM((SLOW + 2, 2 * frames, FAST), F32),
             pltpu.VMEM((512, FAST), F32),
             pltpu.VMEM((512, 8, FAST), BF16),

time: 72.9 us -> 73.8 us (1.012)
  Pallas kernels: 72 us -> 72.8 us
    pallas_call x1, Pallas kernels: 72 us -> 72.8 us  [covariance(): pl.pallas_call(kernel, out_shape=jax.ShapeDtypeStruct((channels, 2, FAST,...]
where the time goes in v6:
time: 73.8 us; the launch traced here: 73.7 us
  Pallas kernels  72.8 us (99%)
  local copies, waits for them, and re-layouts  0.8 us (1%)
    pallas_call x1, Pallas kernels, covariance(): pl.pallas_call(kernel, out_shape=jax.ShapeDtypeStruct((channels, 2, FAST,...  72.8 us

profile of v6, /device:TPU:1, one launch (start us, length us, event | category | flops | bytes accessed | tf_op | source)
XLA Modules:
  0.0 73.7 jit_solution(9162191467134478982)
XLA Ops:
  0.0 72.8 %shard_map.82 = f32[4,2,128,128]{3,2,1,0:T(8,128)S(1)} custom-call(bf16[64,64,128]{2,1,0:T(8,128)(2,1)} %bitcast.5, f32[16,4096]{1,0:T(8,128)} %refs_1_.1, bf16[272,768]{1,0:T(8,128)(2,1)} %constant.6.clone.refs_2_, bf16[128,768]{1,0:T(8,128)(2,1)} %constant.7.clone.refs_3_, f32[4,32,128]{2,1,0:T(8,128)} %constant.8.clone.refs_4_, f32[8,128]{1,0:T(8,128)} %refs_5_.1, ...), custom_call_target="tpu_custom_call" | custom-call | flops 1000000000 | bytes 4194304 | tf_op jit(solution)/shard_map/pallas_call | solution.py:367
  72.9 0.8 %copy.11 = f32[4,2,128,128]{3,2,1,0:T(8,128)} copy(f32[4,2,128,128]{3,2,1,0:T(8,128)S(1)} %shard_map.82) | data formatting | bytes 1048576
